TPU v7x, 128 devices: a whole 4x4x4 slice. The times are simulated.
128 devices in a mesh: gx: 16 (over x, z), gy: 8 (over y, core).
Axes of the slice: x: 4, y: 4, z: 4, core: 2. Of those that a mesh axis runs over, the one named last changes fastest.
Arguments:
- guess: float32 [256, 256, 256], P('gx', 'gy'), may hold values from -6 to 6
- right_side: float32 [256, 256, 256], P('gx', 'gy'), may hold values from -6 to 6
- coefficient: float32 [256, 256, 256], P('gx', 'gy'), may hold values from 0.3 to 3
Outputs:
- solution: float32 [256, 256, 256], P('gx', 'gy')
All inputs are finite; a program needn't handle non-finite values.
Results may differ from a plain program's by a relative error of at most 0.0001.
Values sent between devices are 32-bit elements; how exact they have to be, the bound alone decides.
A program may use at most 128 MiB of HBM per device.

v0:
```python
import functools

import jax
import jax.numpy as jnp
from jax import lax
from jax.experimental import pallas as pl
from jax.experimental.pallas import tpu as pltpu
from jax.sharding import PartitionSpec as P

MESH = pl.DeviceIdType.MESH
F32 = jnp.float32
RELAX = 0.7
CHEB = 8
THETA = 1.04
DELTA = 0.96
LANES = 128


def iota(shape, dim):
    return lax.broadcasted_iota(jnp.int32, shape, dim)


class Level:
    def __init__(self, nh, nz, halo, bx, by, rows, total_x, total_y):
        self.nh, self.nz, self.halo, self.bx, self.by = nh, nz, halo, bx, by
        self.rows, self.total_x, self.total_y = rows, total_x, total_y
        self.width = bx + 2 * halo

    def ext(self):
        return pltpu.VMEM((self.width, self.nh, self.rows, LANES), F32)

    def own(self):
        return pltpu.VMEM((self.bx, self.nh, self.by, LANES), F32)


def z_sum(level, v):
    lane = iota(v[0].shape, 2)
    up = [pltpu.roll(a, 1, 2) for a in v]
    down = [pltpu.roll(a, LANES - 1, 2) for a in v]
    if level.nh == 2:
        low = [jnp.where(lane == 0, 0.0, up[0]), jnp.where(lane == 0, up[0], up[1])]
        high = [
            jnp.where(lane == LANES - 1, down[1], down[0]),
            jnp.where(lane == LANES - 1, 0.0, down[1]),
        ]
    elif level.nz == LANES:
        low = [jnp.where(lane == 0, 0.0, up[0])]
        high = [jnp.where(lane == LANES - 1, 0.0, down[0])]
    else:
        low, high = up, down
    return [a + b for a, b in zip(low, high)]


def block(ref, half, x0, cx, r0, n):
    return ref[pl.ds(x0, cx), half, pl.ds(r0, n), :]


def couple(level, v_ref, c_ref, x0, cx, r0, n):
    halves = range(level.nh)
    v = [block(v_ref, h, x0, cx, r0, n) for h in halves]
    c = [block(c_ref, h, x0, cx, r0, n) for h in halves]
    vz = z_sum(level, v)
    uz = z_sum(level, [a * b for a, b in zip(c, v)])
    out = []
    for h in halves:
        sv, su = vz[h], uz[h]
        for dx, dr in ((-1, 0), (1, 0), (0, -1), (0, 1)):
            near = block(v_ref, h, x0 + dx, cx, r0 + dr, n)
            sv = sv + near
            su = su + near * block(c_ref, h, x0 + dx, cx, r0 + dr, n)
        out.append(c[h] * sv + su)
    return v, out


def loop(count, chunk, body):
    steps = count // chunk
    assert steps * chunk == count
    if steps == 1:
        body(0)
    else:
        lax.fori_loop(0, steps, lambda k, _: (body(k * chunk), 0)[1], 0)


def sweep(level, src, dst, c, g, b, rim, r0, n, chunk, dst_x=0, dst_r=0):
    start = level.halo - rim

    def body(k):
        x0 = start + k
        v, t = couple(level, src, c, x0, chunk, r0, n)
        for h in range(level.nh):
            new = (1.0 - RELAX) * v[h] + block(g, h, x0, chunk, r0, n) * (
                t[h] + block(b, h, x0, chunk, r0, n)
            )
            dst[pl.ds(x0 - dst_x, chunk), h, pl.ds(r0 - dst_r, n), :] = new

    loop(level.bx + 2 * rim, chunk, body)


def first_sweep(level, dst, g, b, rim, r0, n, chunk):
    start = level.halo - rim

    def body(k):
        x0 = start + k
        for h in range(level.nh):
            dst[pl.ds(x0, chunk), h, pl.ds(r0, n), :] = block(g, h, x0, chunk, r0, n) * block(
                b, h, x0, chunk, r0, n
            )

    loop(level.bx + 2 * rim, chunk, body)


def setup(level, c, g, d, rim, r0, n, chunk, base_x, base_y, scale=RELAX):
    start = level.halo - rim

    def body(k):
        x0 = start + k
        halves = range(level.nh)
        mid = [block(c, h, x0, chunk, r0, n) for h in halves]
        cz = z_sum(level, mid)
        shape = mid[0].shape
        px = iota(shape, 0) + (base_x + x0 - level.halo)
        py = iota(shape, 1) + (base_y + r0 - 8)
        mask = (px >= 0) & (px < level.total_x) & (py >= 0) & (py < level.total_y)
        if level.nz < LANES:
            mask = mask & (iota(shape, 2) < level.nz)
        for h in halves:
            total = 6.0 * mid[h] + cz[h]
            for dx, dr in ((-1, 0), (1, 0), (0, -1), (0, 1)):
                total = total + block(c, h, x0 + dx, chunk, r0 + dr, n)
            g[pl.ds(x0, chunk), h, pl.ds(r0, n), :] = jnp.where(
                mask, scale / jnp.where(mask, total, 1.0), 0.0
            )

    loop(level.bx + 2 * rim, chunk, body)

    def diagonal(k):
        halves = range(level.nh)
        x0 = level.halo + k
        mid = [block(c, h, x0, chunk, 8, level.by) for h in halves]
        cz = z_sum(level, mid)
        for h in halves:
            total = 6.0 * mid[h] + cz[h]
            for dx, dr in ((-1, 0), (1, 0), (0, -1), (0, 1)):
                total = total + block(c, h, x0 + dx, chunk, 8 + dr, level.by)
            d[pl.ds(k, chunk), h, :, :] = total

    loop(level.bx, chunk, diagonal)


def residual_pairs(level, v_ref, c, b, d, s, keep, twice=False):
    def body(k):
        x0 = level.halo + 2 * k
        v, t = couple(level, v_ref, c, x0, 2, 8, level.by)
        for h in range(level.nh):
            r = block(b, h, x0, 2, 8, level.by) + t[h] - d[pl.ds(2 * k, 2), h, :, :] * v[h]
            s[pl.ds(k, 1), h, pl.ds(0, level.by), :] = r[0:1] + r[1:2]
            if twice:
                s[pl.ds(k, 1), h, pl.ds(level.by, level.by), :] = r[0:1] + r[1:2]
            if keep is not None:
                keep[pl.ds(x0, 2), h, pl.ds(8, level.by), :] = v[h]

    loop(level.bx // 2, 1, body)


def field_pairs(level, ref, s, twice=False):
    def body(k):
        x0 = level.halo + 2 * k
        for h in range(level.nh):
            r = block(ref, h, x0, 1, 8, level.by) + block(ref, h, x0 + 1, 1, 8, level.by)
            s[pl.ds(k, 1), h, pl.ds(0, level.by), :] = r
            if twice:
                s[pl.ds(k, 1), h, pl.ds(level.by, level.by), :] = r

    loop(level.bx // 2, 1, body)


def dot(a, m):
    return jnp.dot(a, m, precision=lax.Precision.HIGHEST, preferred_element_type=F32)


def halve(level, s, weight, rows=None, lane_base=0):
    rows = level.by // 2 if rows is None else rows
    count = level.bx // 2
    row, col = iota((LANES, LANES), 0), iota((LANES, LANES), 1)
    total = None
    for h in range(level.nh):
        pick = (lax.shift_right_logical(row, 1) + (lane_base + h * 64) == col) & (row < level.nz)
        m = jnp.where(pick, weight, 0.0).astype(F32)
        a = s[:, h, pl.ds(0, rows, stride=2), :] + s[:, h, pl.ds(1, rows, stride=2), :]
        part = dot(a.reshape(count * rows, LANES), m)
        total = part if total is None else total + part
    return total.reshape(count, rows, LANES)


def prolong(level, e, ex, er, count, ne, pe, base, dst, x0):
    row, col = iota((LANES, LANES), 0), iota((LANES, LANES), 1)
    coarse = e[pl.ds(ex, count), 0, pl.ds(er, ne), :].reshape(count * ne, LANES)
    for h in range(level.nh):
        m = jnp.where(row == lax.shift_right_logical(col, 1) + h * 64, 1.0, 0.0).astype(F32)
        pe[:, h, :, :] = dot(coarse, m).reshape(count, ne, LANES)


def add_prolonged(level, pe, base, dst, x0, r0, count, ne):
    def body(k):
        for h in range(level.nh):
            fine = pe[k, h, :, :]
            for dx in range(2):
                for dr in range(2):
                    at = (x0 + 2 * k + dx, h, pl.ds(r0 + dr, ne, stride=2), slice(None))
                    dst[at] = base[at] + fine

    loop(count, 1, body)


class Copy:
    def __init__(self, src, dst, target, sends, receives, sems):
        send_sem, recv_sem, index = sems
        self.copy = pltpu.make_async_remote_copy(
            src_ref=src,
            dst_ref=dst,
            send_sem=send_sem.at[index],
            recv_sem=recv_sem.at[index],
            device_id=target,
            device_id_type=MESH,
        )
        self.sends, self.receives = sends, receives

    def start(self):
        pl.when(self.sends)(lambda: self.copy.start())

    def arrive(self):
        pl.when(self.receives)(lambda: self.copy.wait_recv())

    def leave(self):
        pl.when(self.sends)(lambda: self.copy.wait_send())


def kernel(nx, ny, levels, guess, rhs, coef, out, *scratch):
    l0, l1, l2, l3, l4 = levels
    names = iter(scratch)
    take = lambda k: [next(names) for _ in range(k)]
    va0, vb0, vc0, c0, b0, g0, d0, s0, o0, pe0 = take(10)
    va1, vb1, vc1, c1, b1, g1, d1, s1, pe1 = take(9)
    va2, vb2, vc2, c2, b2, g2, d2, s2, pe2 = take(9)
    va3, vb3, c3, b3, g3, d3, s3, pe3 = take(8)
    va4, vb4, c4, q4, d4, res4, e4 = take(7)
    pc, pb, fc, fb = take(4)
    send_sem, recv_sem, gather_send, gather_recv, local_sem = take(5)

    gx, gy = lax.axis_index("gx"), lax.axis_index("gy")
    counter = iter(range(1000))

    def sems():
        return send_sem, recv_sem, next(counter)

    loads = []
    for i, (src, dst) in enumerate(((coef, c0), (guess, va0), (rhs, b0))):
        for h in range(2):
            loads.append(
                pltpu.make_async_copy(
                    src.at[:, :, h * LANES : (h + 1) * LANES],
                    dst.at[l0.halo : l0.halo + l0.bx, h, 8 : 8 + l0.by, :],
                    local_sem.at[2 * i + h],
                )
            )
    for copy in loads:
        copy.start()

    barrier = pltpu.get_barrier_semaphore()
    for k in range(1, nx):
        pl.semaphore_signal(
            barrier, inc=1, device_id=(lax.rem(gx + k, nx), gy), device_id_type=MESH
        )
    for k in range(1, ny):
        pl.semaphore_signal(
            barrier, inc=1, device_id=(gx, lax.rem(gy + k, ny)), device_id_type=MESH
        )

    everything = []

    class Exchange:
        def __init__(self, level, ref, wide, reach=1, faces=True):
            lo, bx, by = level.halo, level.bx, level.by
            if reach == 1:
                up = ((lo + bx - wide, lo - wide), (lo, lo + bx))
            else:
                up = ((lo + 2 * bx - lo, 0), (lo, lo + 2 * bx))
            self.x, self.y, self.corners = [], [], []
            own = pl.ds(8, by)
            for sign, (src, dst) in zip((1, -1), up):
                there, back = gx + sign * reach, gx - sign * reach
                ok = lambda p: (p >= 0) & (p < nx)
                self.x.append(
                    Copy(
                        ref.at[pl.ds(src, wide), :, own, :],
                        ref.at[pl.ds(dst, wide), :, own, :],
                        (there, gy),
                        ok(there),
                        ok(back),
                        sems(),
                    )
                )
            sides = ((1, by, 0), (-1, 8, 8 + by))
            for sign, src, dst in sides:
                there, back = gy + sign, gy - sign
                ok_y = lambda p: (p >= 0) & (p < ny)
                spans = [(lo, bx, None)] if faces else []
                spans += [(up[0][1], wide, gx - reach >= 0), (up[1][1], wide, gx + reach < nx)]
                for start, count, also in spans:
                    sends, receives = ok_y(there), ok_y(back)
                    if also is not None:
                        sends, receives = sends & also, receives & also
                    (self.y if also is None else self.corners).append(
                        Copy(
                            ref.at[pl.ds(start, count), :, pl.ds(src, 8), :],
                            ref.at[pl.ds(start, count), :, pl.ds(dst, 8), :],
                            (gx, there),
                            sends,
                            receives,
                            sems(),
                        )
                    )
            everything.append(self)

        def send(self):
            for copy in self.x + self.y:
                copy.start()

        def forward(self):
            for copy in self.x:
                copy.arrive()
            for copy in self.corners:
                copy.start()

        def finish(self):
            for copy in self.y + self.corners:
                copy.arrive()

        def leave(self):
            everything.remove(self)
            for copy in self.x + self.y + self.corners:
                copy.leave()

    class Gather:
        def __init__(self, rows, full, index):
            self.rows, self.full = rows, full
            self.first, self.second = [], []
            for k in range(1, ny):
                self.first.append(
                    pltpu.make_async_remote_copy(
                        src_ref=rows.at[gy],
                        dst_ref=rows.at[gy],
                        send_sem=gather_send.at[index, k],
                        recv_sem=gather_recv.at[index, k],
                        device_id=(gx, lax.rem(gy + k, ny)),
                        device_id_type=MESH,
                    )
                )
            mine = full.at[pl.ds(2 * gx, 2)]
            for k in range(1, nx):
                self.second.append(
                    pltpu.make_async_remote_copy(
                        src_ref=mine,
                        dst_ref=mine,
                        send_sem=gather_send.at[index, ny + k],
                        recv_sem=gather_recv.at[index, ny + k],
                        device_id=(lax.rem(gx + k, nx), gy),
                        device_id_type=MESH,
                    )
                )

        def send(self, tile):
            self.rows[gy] = tile
            for copy in self.first:
                copy.start()

        def forward(self):
            for copy in self.first:
                copy.wait_recv()
            total = self.rows[0]
            for k in range(1, ny):
                total = total + self.rows[k]
            self.full[pl.ds(2 * gx, 2)] = total
            for copy in self.second:
                copy.start()

        def finish(self):
            for copy in self.second:
                copy.wait_recv()

        def leave(self):
            for copy in self.first + self.second:
                copy.wait_send()

    x_v0, x_c0, x_b0 = Exchange(l0, va0, 4), Exchange(l0, c0, 4), Exchange(l0, b0, 3)
    x_k0 = Exchange(l0, vc0, 3)
    x_c1, x_b1, x_k1 = Exchange(l1, c1, 5), Exchange(l1, b1, 4), Exchange(l1, vc1, 5)
    x_c2, x_b2, x_k2 = (Exchange(l2, ref, 4) for ref in (c2, b2, vc2))
    f_c2, f_b2, f_k2 = (Exchange(l2, ref, 2, 2, False) for ref in (c2, b2, vc2))
    g_c3, g_b3 = Gather(pc, fc, 0), Gather(pb, fb, 1)

    for copy in loads:
        copy.wait()
    pl.semaphore_wait(barrier, nx + ny - 2)

    x_c0.send()
    x_v0.send()

    def double(k):
        for h in range(2):
            own = (pl.ds(l0.halo + k, 1), h, pl.ds(8, l0.by), slice(None))
            b0[own] = 2.0 * b0[own]

    loop(l0.bx, 1, double)
    x_b0.send()

    def clear(level, refs, far):
        lo, bx, by = level.halo, level.bx, level.by

        def layers(start, count):
            for ref in refs:
                ref[pl.ds(start, count)] = jnp.zeros((count,) + ref.shape[1:], F32)

        near = min(lo, bx)
        pl.when(gx == 0)(lambda: layers(lo - near, near))
        pl.when(gx == nx - 1)(lambda: layers(lo + bx, near))
        if far:
            pl.when(gx < 2)(lambda: layers(0, lo - bx))
            pl.when(gx >= nx - 2)(lambda: layers(lo + 2 * bx, lo - bx))

        def rows(start, count):
            for ref in refs:
                for h in range(level.nh):
                    ref[:, h, pl.ds(start, count), :] = jnp.zeros((level.width, count, LANES), F32)

        pl.when(gy == 0)(lambda: rows(0, 8))
        pl.when(gy == ny - 1)(lambda: rows(8 + by, 8))

    clear(l0, (va0, c0, b0, vc0), False)
    clear(l1, (c1, b1, vc1), False)
    clear(l2, (c2, b2, vc2), True)
    for ref in (vb0, va1, vb1, va2, vb2, va3, vb3, c3, va4, vb4, c4):
        for h in range(ref.shape[1]):
            for r in range(0, ref.shape[2], 8):
                ref[:, h, pl.ds(r, 8), :] = jnp.zeros((ref.shape[0], 8, LANES), F32)

    lane_base = 32 * lax.shift_right_logical(gy, 1)
    odd_rows = iota((2, 8, LANES), 1) >= 4
    mine = odd_rows == ((gy & 1) == 1)

    def tile_of(value):
        return jnp.where(mine, value, 0.0)

    field_pairs(l0, c0, s0)
    c1[l1.halo : l1.halo + l1.bx, 0, 8 : 8 + l1.by, :] = halve(l0, s0, 0.125)
    x_c1.send()
    field_pairs(l1, c1, s1)
    c2[l2.halo : l2.halo + l2.bx, 0, 8 : 8 + l2.by, :] = halve(l1, s1, 0.125)
    x_c2.send()
    f_c2.send()
    field_pairs(l2, c2, s2, True)
    g_c3.send(tile_of(halve(l2, s2, 0.125, 8, lane_base)))

    for exchange in (x_c0, x_v0, x_b0):
        exchange.forward()
    for exchange in (x_c0, x_v0, x_b0):
        exchange.finish()
    bx0, by0 = gx * l0.bx, gy * l0.by

    setup(l0, c0, g0, d0, 3, 4, 40, 1, bx0, by0)
    sweep(l0, va0, vb0, c0, g0, b0, 3, 4, 40, 1)
    x_v0.leave()
    sweep(l0, vb0, va0, c0, g0, b0, 2, 4, 40, 1)
    sweep(l0, va0, vb0, c0, g0, b0, 1, 4, 40, 1)
    residual_pairs(l0, vb0, c0, b0, d0, s0, vc0)
    b1[l1.halo : l1.halo + l1.bx, 0, 8 : 8 + l1.by, :] = halve(l0, s0, 0.5)
    x_b1.send()
    x_k0.send()
    for exchange in (x_c1, x_c2, f_c2):
        exchange.forward()
    g_c3.forward()
    for exchange in (x_c1, x_c2, f_c2):
        exchange.finish()
    setup(l1, c1, g1, d1, 4, 4, 24, 2, gx * l1.bx, gy * l1.by)
    setup(l2, c2, g2, d2, 5, 2, 24, 2, gx * l2.bx, gy * l2.by)
    x_b1.forward()
    x_b1.finish()
    first_sweep(l1, va1, g1, b1, 3, 4, 24, 2)
    sweep(l1, va1, vb1, c1, g1, b1, 2, 4, 24, 2)
    sweep(l1, vb1, va1, c1, g1, b1, 1, 4, 24, 2)
    residual_pairs(l1, va1, c1, b1, d1, s1, vc1)
    b2[l2.halo : l2.halo + l2.bx, 0, 8 : 8 + l2.by, :] = halve(l1, s1, 0.5)
    x_b2.send()
    f_b2.send()
    x_k1.send()

    def unpack(packed, dst):
        def body(k):
            t = packed[pl.ds(k, 4)]
            lane = iota(t.shape, 2)
            for q in range(l3.total_y // 8):
                part = t if q == 0 else pltpu.roll(t, LANES - 32 * q, 2)
                dst[pl.ds(l3.halo + k, 4), 0, pl.ds(8 + 8 * q, 8), :] = jnp.where(
                    lane < 32, part, 0.0
                )

        loop(l3.bx, 4, body)

    g_c3.finish()
    unpack(fc, c3)
    setup(l3, c3, g3, d3, 0, 8, l3.by, 2, 0, 0)
    field_pairs(l3, c3, s3)
    c4[l4.halo : l4.halo + l4.bx, 0, 8 : 8 + l4.by, :] = halve(l3, s3, 0.125)
    setup(l4, c4, q4, d4, 0, 8, l4.by, 2, 0, 0, 1.0)

    x_b2.forward()
    x_b2.finish()
    first_sweep(l2, va2, g2, b2, 3, 2, 24, 2)
    sweep(l2, va2, vb2, c2, g2, b2, 2, 2, 24, 2)
    sweep(l2, vb2, va2, c2, g2, b2, 1, 2, 24, 2)
    residual_pairs(l2, va2, c2, b2, d2, s2, vc2, True)
    g_b3.send(tile_of(halve(l2, s2, 0.5, 8, lane_base)))
    x_k2.send()
    f_k2.send()
    x_k0.forward()
    x_k1.forward()
    f_b2.forward()
    g_b3.forward()
    x_k2.forward()
    f_k2.forward()
    g_b3.finish()
    unpack(fb, b3)

    first_sweep(l3, va3, g3, b3, 0, 8, l3.by, 2)
    sweep(l3, va3, vb3, c3, g3, b3, 0, 8, l3.by, 2)
    sweep(l3, vb3, va3, c3, g3, b3, 0, 8, l3.by, 2)
    residual_pairs(l3, va3, c3, b3, d3, s3, None)

    res4[:, 0, :, :] = halve(l3, s3, 0.5)
    sigma = THETA / DELTA
    rho = 1.0 / sigma
    inner = (pl.ds(l4.halo, l4.bx), 0, pl.ds(8, l4.by), slice(None))
    q = q4[inner]
    direction = res4[:, 0, :, :] * q * (1.0 / THETA)
    e4[:, 0, :, :] = direction
    va4[inner] = direction
    src, dst = va4, vb4
    for step in range(CHEB - 1):
        v, t = couple(l4, src, c4, l4.halo, l4.bx, 8, l4.by)
        r = res4[:, 0, :, :] - (d4[:, 0, :, :] * v[0] - t[0])
        rho_new = 1.0 / (2.0 * sigma - rho)
        direction = (rho_new * rho) * v[0] + (2.0 * rho_new / DELTA) * (r * q4[inner])
        rho = rho_new
        res4[:, 0, :, :] = r
        e4[:, 0, :, :] = e4[:, 0, :, :] + direction
        dst[inner] = direction
        src, dst = dst, src

    prolong(l3, e4, 0, 0, l4.bx, l4.by, pe3, None, None, 0)
    add_prolonged(l3, pe3, va3, vb3, l3.halo, 8, l4.bx, l4.by)
    sweep(l3, vb3, va3, c3, g3, b3, 0, 8, l3.by, 2)
    sweep(l3, va3, vb3, c3, g3, b3, 0, 8, l3.by, 2)
    sweep(l3, vb3, va3, c3, g3, b3, 0, 8, l3.by, 2)

    f_b2.finish()
    x_k2.finish()
    f_k2.finish()
    prolong(l2, va3, 2 * gx + 1, 4 * gy + 4, 8, 16, pe2, None, None, 0)
    add_prolonged(l2, pe2, vc2, va2, 0, 0, 8, 16)
    sweep(l2, va2, vb2, c2, g2, b2, 5, 2, 24, 2)
    sweep(l2, vb2, va2, c2, g2, b2, 4, 2, 24, 2)
    sweep(l2, va2, vb2, c2, g2, b2, 3, 2, 24, 2)

    x_k1.finish()
    prolong(l1, vb2, 3, 4, 10, 16, pe1, None, None, 0)
    add_prolonged(l1, pe1, vc1, va1, 0, 0, 10, 16)
    sweep(l1, va1, vb1, c1, g1, b1, 4, 4, 24, 2)
    sweep(l1, vb1, va1, c1, g1, b1, 3, 4, 24, 2)
    sweep(l1, va1, vb1, c1, g1, b1, 2, 4, 24, 2)

    x_k0.finish()
    prolong(l0, vb1, 4, 4, 12, 24, pe0, None, None, 0)
    add_prolonged(l0, pe0, vc0, va0, 0, 0, 12, 24)
    sweep(l0, va0, vb0, c0, g0, b0, 2, 4, 40, 1)
    sweep(l0, vb0, va0, c0, g0, b0, 1, 4, 40, 1)
    sweep(l0, va0, o0, c0, g0, b0, 0, 8, 32, 1, l0.halo, 8)
    stores = []
    for h in range(2):
        stores.append(
            pltpu.make_async_copy(
                o0.at[:, h], out.at[:, :, h * LANES : (h + 1) * LANES], local_sem.at[6 + h]
            )
        )
    for copy in stores:
        copy.start()
    for copy in stores:
        copy.wait()
    for exchange in list(everything):
        exchange.leave()
    g_c3.leave()
    g_b3.leave()


def solution(mesh):
    nx, ny = mesh.shape["gx"], mesh.shape["gy"]
    l0 = Level(2, 256, 4, 16, 32, 48, 16 * nx, 32 * ny)
    l1 = Level(1, 128, 6, 8, 16, 32, 8 * nx, 16 * ny)
    l2 = Level(1, 64, 6, 4, 8, 32, 4 * nx, 8 * ny)
    l3 = Level(1, 32, 4, 2 * nx, 4 * ny, 16 + 4 * ny, 2 * nx, 4 * ny)
    l4 = Level(1, 16, 1, nx, 2 * ny, 16 + 2 * ny, nx, 2 * ny)

    def vmem(*shape):
        return pltpu.VMEM(shape, F32)

    e, o = (lambda l: l.ext()), (lambda l: l.own())
    scratch = [e(l0)] * 6 + [o(l0), vmem(8, 2, 32, LANES), o(l0), vmem(12, 2, 24, LANES)]
    scratch += [e(l1)] * 6 + [o(l1), vmem(4, 1, 16, LANES), vmem(10, 1, 16, LANES)]
    scratch += [e(l2)] * 6 + [o(l2), vmem(2, 1, 16, LANES), vmem(8, 1, 16, LANES)]
    scratch += [e(l3)] * 5 + [o(l3), vmem(nx, 1, 4 * ny, LANES), vmem(nx, 1, 2 * ny, LANES)]
    scratch += [e(l4)] * 4 + [o(l4)] * 3
    scratch += [vmem(ny, 2, 8, LANES)] * 2 + [vmem(2 * nx, 8, LANES)] * 2
    copies = 10 * 8 + 3 * 6
    scratch += [
        pltpu.SemaphoreType.DMA((copies,)),
        pltpu.SemaphoreType.DMA((copies,)),
        pltpu.SemaphoreType.DMA((2, nx + ny)),
        pltpu.SemaphoreType.DMA((2, nx + ny)),
        pltpu.SemaphoreType.DMA((8,)),
    ]

    def step(guess, right_side, coefficient):
        return pl.pallas_call(
            functools.partial(kernel, nx, ny, (l0, l1, l2, l3, l4)),
            out_shape=jax.ShapeDtypeStruct(guess.shape, F32),
            in_specs=[pl.BlockSpec(memory_space=pl.ANY)] * 3,
            out_specs=pl.BlockSpec(memory_space=pl.ANY),
            scratch_shapes=scratch,
            compiler_params=pltpu.CompilerParams(collective_id=0, has_side_effects=True),
        )(guess, right_side, coefficient)

    spec = P("gx", "gy", None)
    return jax.shard_map(
        step, mesh=mesh, in_specs=(spec, spec, spec), out_specs=spec, check_vma=False
    )
```

profile of v0, /device:TPU:0, one launch (start us, length us, event | category | flops | bytes accessed | tf_op | source)
XLA Modules:
  0.0 94.2 jit_solution(12384085362302248839)
XLA Ops:
  0.0 92.3 %shard_map.37 = f32[16,32,256]{2,1,0:T(8,128)} custom-call(f32[16,32,256]{2,1,0:T(8,128)} %guess.1, f32[16,32,256]{2,1,0:T(8,128)} %rhs.1, f32[16,32,256]{2,1,0:T(8,128)} %coef.1), custom_call_target="tpu_custom_call" | custom-call | tf_op jit(solution)/shard_map/pallas_call | solution.py:632
  92.3 1.9 %copy.5 = f32[16,32,256]{2,1,0:T(8,128)} copy(f32[16,32,256]{2,1,0:T(8,128)} %shard_map.37) | data formatting | bytes 1048576
where the time goes:
time: 94.3 us; the launch traced here: 94.2 us
  Pallas kernels  92.3 us (98%)
  local copies, waits for them, and re-layouts  1.88 us (2%)
    pallas_call x1, Pallas kernels, step(): pl.pallas_call(functools.partial(kernel, nx, ny, (l0, l1, l2, l3, l4)), o...  92.3 us

commit v1 on v0

v1 whole, which is shorter than its diff:
```python
import functools

import jax
import jax.numpy as jnp
from jax import lax
from jax.experimental import pallas as pl
from jax.experimental.pallas import tpu as pltpu
from jax.sharding import PartitionSpec as P

MESH = pl.DeviceIdType.MESH
F32 = jnp.float32
RELAX = 0.7
CHEB = 8
THETA = 1.04
DELTA = 0.96
LANES = 128


def iota(shape, dim):
    return lax.broadcasted_iota(jnp.int32, shape, dim)


class Level:
    def __init__(self, nh, nz, halo, bx, by, rows, total_x, total_y):
        self.nh, self.nz, self.halo, self.bx, self.by = nh, nz, halo, bx, by
        self.rows, self.total_x, self.total_y = rows, total_x, total_y
        self.width = bx + 2 * halo

    def ext(self):
        return pltpu.VMEM((self.width, self.nh, self.rows, LANES), F32)

    def own(self):
        return pltpu.VMEM((self.bx, self.nh, self.by, LANES), F32)


def z_sum(level, v):
    lane = iota(v[0].shape, 2)
    up = [pltpu.roll(a, 1, 2) for a in v]
    down = [pltpu.roll(a, LANES - 1, 2) for a in v]
    if level.nh == 2:
        low = [jnp.where(lane == 0, 0.0, up[0]), jnp.where(lane == 0, up[0], up[1])]
        high = [
            jnp.where(lane == LANES - 1, down[1], down[0]),
            jnp.where(lane == LANES - 1, 0.0, down[1]),
        ]
    elif level.nz == LANES:
        low = [jnp.where(lane == 0, 0.0, up[0])]
        high = [jnp.where(lane == LANES - 1, 0.0, down[0])]
    else:
        low, high = up, down
    return [a + b for a, b in zip(low, high)]


def block(ref, half, x0, cx, r0, n):
    return ref[pl.ds(x0, cx), half, pl.ds(r0, n), :]


def couple(level, v_ref, c_ref, x0, cx, r0, n):
    halves = range(level.nh)
    v = [block(v_ref, h, x0, cx, r0, n) for h in halves]
    c = [block(c_ref, h, x0, cx, r0, n) for h in halves]
    vz = z_sum(level, v)
    uz = z_sum(level, [a * b for a, b in zip(c, v)])
    out = []
    for h in halves:
        sv, su = vz[h], uz[h]
        for dx, dr in ((-1, 0), (1, 0), (0, -1), (0, 1)):
            near = block(v_ref, h, x0 + dx, cx, r0 + dr, n)
            sv = sv + near
            su = su + near * block(c_ref, h, x0 + dx, cx, r0 + dr, n)
        out.append(c[h] * sv + su)
    return v, out


def pieces(x0, count, r0, n):
    return [(x0 + i, r0 + r) for i in range(count) for r in range(0, n, 8)]


def loop(count, chunk, body):
    steps = count // chunk
    assert steps * chunk == count
    if steps == 1:
        body(0)
    else:
        lax.fori_loop(0, steps, lambda k, _: (body(k * chunk), 0)[1], 0)


def sweep(level, src, dst, c, g, b, rim, r0, n, chunk, dst_x=0, dst_r=0):
    start = level.halo - rim
    chunk = chunk or (level.bx + 2 * rim) // 2

    def body(k):
        for x0, r in pieces(start + k, chunk, r0, n):
            v, t = couple(level, src, c, x0, 1, r, 8)
            for h in range(level.nh):
                new = (1.0 - RELAX) * v[h] + block(g, h, x0, 1, r, 8) * (
                    t[h] + block(b, h, x0, 1, r, 8)
                )
                dst[pl.ds(x0 - dst_x, 1), h, pl.ds(r - dst_r, 8), :] = new

    loop(level.bx + 2 * rim, chunk, body)


def first_sweep(level, dst, g, b, rim, r0, n, chunk):
    start = level.halo - rim
    chunk = chunk or (level.bx + 2 * rim) // 2

    def body(k):
        x0 = start + k
        for h in range(level.nh):
            dst[pl.ds(x0, chunk), h, pl.ds(r0, n), :] = block(g, h, x0, chunk, r0, n) * block(
                b, h, x0, chunk, r0, n
            )

    loop(level.bx + 2 * rim, chunk, body)


def setup(level, c, g, d, rim, r0, n, chunk, base_x, base_y, scale=RELAX):
    start = level.halo - rim

    def body(k):
        halves = range(level.nh)
        for x0, r in pieces(start + k, chunk, r0, n):
            mid = [block(c, h, x0, 1, r, 8) for h in halves]
            cz = z_sum(level, mid)
            shape = mid[0].shape
            px = base_x + x0 - level.halo
            py = iota(shape, 1) + jnp.where((px >= 0) & (px < level.total_x), base_y + r - 8, -1000)
            mask = (py >= 0) & (py < level.total_y)
            if level.nz < LANES:
                mask = mask & (iota(shape, 2) < level.nz)
            for h in halves:
                total = 6.0 * mid[h] + cz[h]
                for dx, dr in ((-1, 0), (1, 0), (0, -1), (0, 1)):
                    total = total + block(c, h, x0 + dx, 1, r + dr, 8)
                g[pl.ds(x0, 1), h, pl.ds(r, 8), :] = jnp.where(
                    mask, scale / jnp.where(mask, total, 1.0), 0.0
                )

    loop(level.bx + 2 * rim, chunk, body)

    def diagonal(k):
        halves = range(level.nh)
        for x0, r in pieces(level.halo + k, chunk, 8, level.by):
            mid = [block(c, h, x0, 1, r, 8) for h in halves]
            cz = z_sum(level, mid)
            for h in halves:
                total = 6.0 * mid[h] + cz[h]
                for dx, dr in ((-1, 0), (1, 0), (0, -1), (0, 1)):
                    total = total + block(c, h, x0 + dx, 1, r + dr, 8)
                d[pl.ds(x0 - level.halo, 1), h, pl.ds(r - 8, 8), :] = total

    loop(level.bx, chunk, diagonal)


def residual_pairs(level, v_ref, c, b, d, s, keep):
    def body(k):
        for r in range(0, level.by, 8):
            parts = []
            for dx in range(2):
                x0 = level.halo + 2 * k + dx
                v, t = couple(level, v_ref, c, x0, 1, 8 + r, 8)
                for h in range(level.nh):
                    own = d[pl.ds(2 * k + dx, 1), h, pl.ds(r, 8), :]
                    parts.append(block(b, h, x0, 1, 8 + r, 8) + t[h] - own * v[h])
                    if keep is not None:
                        keep[pl.ds(x0, 1), h, pl.ds(8 + r, 8), :] = v[h]
            for h in range(level.nh):
                total = parts[h] + parts[level.nh + h]
                s[pl.ds(k, 1), h, pl.ds(r, 8), :] = total

    loop(level.bx // 2, 1, body)


def field_pairs(level, ref, s):
    def body(k):
        x0 = level.halo + 2 * k
        for h in range(level.nh):
            r = block(ref, h, x0, 1, 8, level.by) + block(ref, h, x0 + 1, 1, 8, level.by)
            s[pl.ds(k, 1), h, pl.ds(0, level.by), :] = r

    loop(level.bx // 2, 1, body)


def dot(a, m):
    return jnp.dot(a, m, precision=lax.Precision.HIGHEST, preferred_element_type=F32)


def halve(level, s, weight):
    rows = level.by // 2
    count = level.bx // 2
    row, col = iota((LANES, LANES), 0), iota((LANES, LANES), 1)
    total = None
    for h in range(level.nh):
        pick = (lax.shift_right_logical(row, 1) + h * 64 == col) & (row < level.nz)
        m = jnp.where(pick, weight, 0.0).astype(F32)
        a = s[:, h, pl.ds(0, rows, stride=2), :] + s[:, h, pl.ds(1, rows, stride=2), :]
        part = dot(a.reshape(count * rows, LANES), m)
        total = part if total is None else total + part
    return total.reshape(count, rows, LANES)


def prolong(level, e, ex, er, count, ne, pe, base, dst, x0):
    row, col = iota((LANES, LANES), 0), iota((LANES, LANES), 1)
    coarse = e[pl.ds(ex, count), 0, pl.ds(er, ne), :].reshape(count * ne, LANES)
    for h in range(level.nh):
        m = jnp.where(row == lax.shift_right_logical(col, 1) + h * 64, 1.0, 0.0).astype(F32)
        pe[:, h, :, :] = dot(coarse, m).reshape(count, ne, LANES)


def add_prolonged(level, pe, base, dst, x0, r0, count, ne, er=0):
    def body(k):
        for h in range(level.nh):
            fine = pe[k, h, pl.ds(er, ne), :]
            for dx in range(2):
                for dr in range(2):
                    at = (x0 + 2 * k + dx, h, pl.ds(r0 + dr, ne, stride=2), slice(None))
                    dst[at] = base[at] + fine

    loop(count, 1, body)


class Packed:
    def __init__(self, count, pad, rows, width, groups):
        self.count, self.pad, self.rows, self.width, self.groups = count, pad, rows, width, groups

    def ext(self):
        return pltpu.VMEM((self.count + 2 * self.pad, 8, LANES), F32)

    def own(self, more=0):
        return pltpu.VMEM((self.count + more, 8, LANES), F32)


def packed_near(p, v):
    row = iota(v.shape, 1) & (p.rows - 1)
    after, before = pltpu.roll(v, 7, 1), pltpu.roll(v, 1, 1)
    return (
        jnp.where(row == p.rows - 1, pltpu.roll(after, LANES - p.width, 2), after),
        jnp.where(row == 0, pltpu.roll(before, p.width, 2), before),
        pltpu.roll(v, LANES - 1, 2),
        pltpu.roll(v, 1, 2),
    )


def packed_setup(p, c, w, wx, g, d, scale):
    def body(k):
        at = pl.ds(p.pad + k, 1)
        mid = c[at]
        lane, row = iota(mid.shape, 2), iota(mid.shape, 1) & (p.rows - 1)
        valid = lane < p.width * p.groups
        z = lane & (p.width - 1)
        inside = (
            (row < p.rows - 1) | (lane < p.width * (p.groups - 1)),
            (row > 0) | (lane >= p.width),
            z < p.width - 1,
            z > 0,
        )
        below = c[pl.ds(p.pad + k - 1, 1)]
        total = 6.0 * mid + below + c[pl.ds(p.pad + k + 1, 1)]
        wx[pl.ds(k, 1)] = mid + below
        for ref, near, ok in zip(w, packed_near(p, mid), inside):
            near = jnp.where(valid & ok, near, 0.0)
            ref[pl.ds(k, 1)] = jnp.where(valid & ok, mid + near, 0.0)
            total = total + near
        g[pl.ds(k, 1)] = jnp.where(valid, scale / jnp.where(valid, total, 1.0), 0.0)
        d[pl.ds(k, 1)] = total

    loop_pieces(p.count, 4, body)
    wx[pl.ds(p.count, 1)] = c[pl.ds(p.pad + p.count - 1, 1)]


def packed_couple(p, v_ref, w, wx, k):
    v = v_ref[pl.ds(p.pad + k, 1)]
    t = wx[pl.ds(k, 1)] * v_ref[pl.ds(p.pad + k - 1, 1)]
    t = t + wx[pl.ds(k + 1, 1)] * v_ref[pl.ds(p.pad + k + 1, 1)]
    parts = [ref[pl.ds(k, 1)] * near for ref, near in zip(w, packed_near(p, v))]
    return v, t + ((parts[0] + parts[1]) + (parts[2] + parts[3]))


def loop_pieces(count, chunk, body):
    def several(k):
        for i in range(chunk):
            body(k + i)

    loop(count, chunk, several)


def packed_sweep(p, src, dst, w, wx, g, b, b_pad):
    def body(k):
        v, t = packed_couple(p, src, w, wx, k)
        new = (1.0 - RELAX) * v + g[pl.ds(k, 1)] * (t + b[pl.ds(b_pad + k, 1)])
        dst[pl.ds(p.pad + k, 1)] = new

    loop_pieces(p.count, 16, body)


def packed_halve(s, weight):
    row, col = iota((LANES, LANES), 0), iota((LANES, LANES), 1)
    m = jnp.where(lax.shift_right_logical(row, 1) == col, weight, 0.0).astype(F32)
    a = s[:, pl.ds(0, 8, stride=2), :] + s[:, pl.ds(1, 8, stride=2), :]
    return dot(a.reshape(s.shape[0] * 8, LANES), m).reshape(s.shape[0], 8, LANES)


class Copy:
    def __init__(self, src, dst, target, sends, receives, sems):
        send_sem, recv_sem, index = sems
        self.copy = pltpu.make_async_remote_copy(
            src_ref=src,
            dst_ref=dst,
            send_sem=send_sem.at[index],
            recv_sem=recv_sem.at[index],
            device_id=target,
            device_id_type=MESH,
        )
        self.sends, self.receives = sends, receives

    def start(self):
        pl.when(self.sends)(lambda: self.copy.start())

    def arrive(self):
        pl.when(self.receives)(lambda: self.copy.wait_recv())

    def leave(self):
        pl.when(self.sends)(lambda: self.copy.wait_send())


def kernel(nx, ny, levels, guess, rhs, coef, out, *scratch):
    l0, l1, l2, l3, l4 = levels
    names = iter(scratch)
    take = lambda k: [next(names) for _ in range(k)]
    va0, vb0, vc0, c0, b0, g0, d0, s0, o0, pe0 = take(10)
    va1, vb1, vc1, c1, b1, g1, d1, s1, pe1 = take(9)
    va2, vb2, vc2, c2, b2, g2, d2, s2, pe2 = take(9)
    va3, vb3, c3, b3, wx3, g3, d3, s3, t3 = take(9)
    w3 = take(4)
    va4, vb4, c4, wx4, q4, d4, res4, e4 = take(8)
    w4 = take(4)
    pc, pb = take(2)
    send_sem, recv_sem, gather_send, gather_recv, local_sem = take(5)

    gx, gy = lax.axis_index("gx"), lax.axis_index("gy")
    counter = iter(range(1000))

    def sems():
        return send_sem, recv_sem, next(counter)

    loads = []
    for i, (src, dst) in enumerate(((coef, c0), (guess, va0), (rhs, b0))):
        for h in range(2):
            loads.append(
                pltpu.make_async_copy(
                    src.at[:, :, h * LANES : (h + 1) * LANES],
                    dst.at[l0.halo : l0.halo + l0.bx, h, 8 : 8 + l0.by, :],
                    local_sem.at[2 * i + h],
                )
            )
    for copy in loads:
        copy.start()

    barrier = pltpu.get_barrier_semaphore()
    for k in range(1, nx):
        pl.semaphore_signal(
            barrier, inc=1, device_id=(lax.rem(gx + k, nx), gy), device_id_type=MESH
        )
    for k in range(1, ny):
        pl.semaphore_signal(
            barrier, inc=1, device_id=(gx, lax.rem(gy + k, ny)), device_id_type=MESH
        )

    everything = []

    class Exchange:
        def __init__(self, level, ref, wide, reach=1, faces=True):
            lo, bx, by = level.halo, level.bx, level.by
            if reach == 1:
                up = ((lo + bx - wide, lo - wide), (lo, lo + bx))
            else:
                up = ((lo + 2 * bx - lo, 0), (lo, lo + 2 * bx))
            self.x, self.y, self.corners = [], [], []
            own = pl.ds(8, by)
            for sign, (src, dst) in zip((1, -1), up):
                there, back = gx + sign * reach, gx - sign * reach
                ok = lambda p: (p >= 0) & (p < nx)
                self.x.append(
                    Copy(
                        ref.at[pl.ds(src, wide), :, own, :],
                        ref.at[pl.ds(dst, wide), :, own, :],
                        (there, gy),
                        ok(there),
                        ok(back),
                        sems(),
                    )
                )
            rows = 4 if level.nh == 2 else 8
            sides = ((1, 8 + by - rows, 8 - rows), (-1, 8, 8 + by))
            for sign, src, dst in sides:
                there, back = gy + sign, gy - sign
                ok_y = lambda p: (p >= 0) & (p < ny)
                spans = [(lo, bx, None)] if faces else []
                spans += [(up[0][1], wide, gx - reach >= 0), (up[1][1], wide, gx + reach < nx)]
                for start, count, also in spans:
                    sends, receives = ok_y(there), ok_y(back)
                    if also is not None:
                        sends, receives = sends & also, receives & also
                    (self.y if also is None else self.corners).append(
                        Copy(
                            ref.at[pl.ds(start, count), :, pl.ds(src, rows), :],
                            ref.at[pl.ds(start, count), :, pl.ds(dst, rows), :],
                            (gx, there),
                            sends,
                            receives,
                            sems(),
                        )
                    )
            everything.append(self)

        def send(self):
            for copy in self.x + self.y:
                copy.start()

        def forward(self):
            for copy in self.x:
                copy.arrive()
            for copy in self.corners:
                copy.start()

        def finish(self):
            for copy in self.y + self.corners:
                copy.arrive()

        def leave(self):
            everything.remove(self)
            for copy in self.x + self.y + self.corners:
                copy.leave()

    class Gather:
        def __init__(self, rows, full, pad, index):
            self.rows, self.full, self.at = rows, full, pl.ds(pad + 2 * gx, 2)
            self.first = [
                self.copy(rows.at[gy], index, (gx, lax.rem(gy + k, ny))) for k in range(1, ny)
            ]
            mine = full.at[self.at]
            self.second = [
                self.copy(mine, index + 1, (lax.rem(gx + k, nx), gy)) for k in range(1, nx)
            ]
            self.first_all = self.copy(rows.at[pl.ds(0, ny - 1)], index, (gx, gy))
            self.second_all = self.copy(full.at[pl.ds(0, 2 * nx - 2)], index + 1, (gx, gy))

        def copy(self, ref, index, target):
            return pltpu.make_async_remote_copy(
                src_ref=ref,
                dst_ref=ref,
                send_sem=gather_send.at[index],
                recv_sem=gather_recv.at[index],
                device_id=target,
                device_id_type=MESH,
            )

        def send(self, tile):
            self.rows[gy] = tile
            for copy in self.first:
                copy.start()

        def forward(self):
            self.first_all.wait_recv()
            even, odd = self.rows[0], self.rows[1]
            for k in range(2, ny, 2):
                even, odd = even + self.rows[k], odd + self.rows[k + 1]
            low = iota(even.shape, 0) < 4
            layers = (
                jnp.where(low, even, pltpu.roll(odd, 4, 0)),
                jnp.where(low, pltpu.roll(even, 4, 0), odd),
            )
            for i in range(2):
                self.full[self.at.start + i] = layers[i]
            for copy in self.second:
                copy.start()

        def finish(self):
            self.second_all.wait_recv()

        def leave(self):
            self.first_all.wait_send()
            self.second_all.wait_send()

    x_v0, x_c0, x_b0 = Exchange(l0, va0, 4), Exchange(l0, c0, 4), Exchange(l0, b0, 3)
    x_k0 = Exchange(l0, vc0, 3)
    x_c1, x_b1, x_k1 = Exchange(l1, c1, 5), Exchange(l1, b1, 4), Exchange(l1, vc1, 5)
    x_c2, x_b2, x_k2 = (Exchange(l2, ref, 4) for ref in (c2, b2, vc2))
    f_c2, f_b2, f_k2 = (Exchange(l2, ref, 2, 2, False) for ref in (c2, b2, vc2))
    g_c3, g_b3 = Gather(pc, c3, l3.pad, 0), Gather(pb, b3, l3.pad, 2)

    for copy in loads:
        copy.wait()
    pl.semaphore_wait(barrier, nx + ny - 2)

    x_c0.send()
    x_v0.send()

    def double(k):
        for h in range(2):
            own = (pl.ds(l0.halo + k, 1), h, pl.ds(8, l0.by), slice(None))
            b0[own] = 2.0 * b0[own]

    loop(l0.bx, 1, double)
    x_b0.send()

    def clear(level, refs, far):
        lo, bx, by = level.halo, level.bx, level.by

        def layers(start, count):
            for ref in refs:
                ref[pl.ds(start, count)] = jnp.zeros((count,) + ref.shape[1:], F32)

        near = min(lo, bx)
        pl.when(gx == 0)(lambda: layers(lo - near, near))
        pl.when(gx == nx - 1)(lambda: layers(lo + bx, near))
        if far:
            pl.when(gx < 2)(lambda: layers(0, lo - bx))
            pl.when(gx >= nx - 2)(lambda: layers(lo + 2 * bx, lo - bx))

        def rows(start, count):
            for ref in refs:
                for h in range(level.nh):
                    ref[:, h, pl.ds(start, count), :] = jnp.zeros((level.width, count, LANES), F32)

        pl.when(gy == 0)(lambda: rows(0, 8))
        pl.when(gy == ny - 1)(lambda: rows(8 + by, 8))

    clear(l0, (va0, c0, b0, vc0), False)
    clear(l1, (c1, b1, vc1), False)
    clear(l2, (c2, b2, vc2), True)
    for ref in (va3, vb3, c3, va4, vb4, c4):
        pad = 1 if ref.shape[0] == nx + 2 else l3.pad
        for start in (0, ref.shape[0] - pad):
            ref[pl.ds(start, pad)] = jnp.zeros((pad, 8, LANES), F32)
    for ref in (vb0, va1, vb1, va2, vb2):
        for h in range(ref.shape[1]):
            for r in range(0, ref.shape[2], 8):
                ref[:, h, pl.ds(r, 8), :] = jnp.zeros((ref.shape[0], 8, LANES), F32)

    lane_base = 32 * lax.shift_right_logical(gy, 1)

    def tile_of(s, weight):
        row, col = iota((LANES, LANES), 0), iota((LANES, LANES), 1)
        pick = (lax.shift_right_logical(row, 1) + lane_base == col) & (row < l2.nz)
        m = jnp.where(pick, weight, 0.0).astype(F32)
        a = s[pl.ds(0, 8, stride=2), :] + s[pl.ds(1, 8, stride=2), :]
        return dot(a, m)

    field_pairs(l0, c0, s0)
    c1[l1.halo : l1.halo + l1.bx, 0, 8 : 8 + l1.by, :] = halve(l0, s0, 0.125)
    x_c1.send()
    field_pairs(l1, c1, s1)
    c2[l2.halo : l2.halo + l2.bx, 0, 8 : 8 + l2.by, :] = halve(l1, s1, 0.125)
    x_c2.send()
    f_c2.send()
    for k in range(2):
        s2[pl.ds(8 * k, 8), :] = (
            c2[l2.halo + 2 * k, 0, pl.ds(8, 8), :] + c2[l2.halo + 2 * k + 1, 0, pl.ds(8, 8), :]
        )
    g_c3.send(tile_of(s2, 0.125))

    for exchange in (x_c0, x_v0, x_b0):
        exchange.forward()
    for exchange in (x_c0, x_v0, x_b0):
        exchange.finish()
    g_c3.forward()
    for exchange in (x_c1, x_c2, f_c2):
        exchange.forward()
    bx0, by0 = gx * l0.bx, gy * l0.by

    setup(l0, c0, g0, d0, 3, 4, 40, 2, bx0, by0)
    sweep(l0, va0, vb0, c0, g0, b0, 3, 4, 40, 2)
    x_v0.leave()
    sweep(l0, vb0, va0, c0, g0, b0, 2, 4, 40, 2)
    sweep(l0, va0, vb0, c0, g0, b0, 1, 4, 40, 2)
    residual_pairs(l0, vb0, c0, b0, d0, s0, vc0)
    b1[l1.halo : l1.halo + l1.bx, 0, 8 : 8 + l1.by, :] = halve(l0, s0, 0.5)
    x_b1.send()
    x_k0.send()
    for exchange in (x_c1, x_c2, f_c2):
        exchange.finish()
    setup(l1, c1, g1, d1, 4, 4, 24, 2, gx * l1.bx, gy * l1.by)
    setup(l2, c2, g2, d2, 5, 2, 24, 2, gx * l2.bx, gy * l2.by)
    x_b1.forward()
    x_b1.finish()
    first_sweep(l1, va1, g1, b1, 3, 4, 24, 0)
    sweep(l1, va1, vb1, c1, g1, b1, 2, 4, 24, 0)
    sweep(l1, vb1, va1, c1, g1, b1, 1, 4, 24, 0)
    residual_pairs(l1, va1, c1, b1, d1, s1, vc1)
    b2[l2.halo : l2.halo + l2.bx, 0, 8 : 8 + l2.by, :] = halve(l1, s1, 0.5)
    x_b2.send()
    f_b2.send()
    x_k1.send()

    def pairs_of(ref):
        for k in range(nx):
            total = ref[l3.pad + 2 * k] + ref[l3.pad + 2 * k + 1]
            s3[k, pl.ds(0, 8), :] = total
            s3[k, pl.ds(8, 8), :] = total

    g_c3.finish()
    packed_setup(l3, c3, w3, wx3, g3, d3, RELAX)
    pairs_of(c3)
    c4[pl.ds(l4.pad, nx)] = packed_halve(s3, 0.125)
    packed_setup(l4, c4, w4, wx4, q4, d4, 1.0)

    x_b2.forward()
    x_b2.finish()
    first_sweep(l2, va2, g2, b2, 3, 2, 24, 0)
    sweep(l2, va2, vb2, c2, g2, b2, 2, 2, 24, 0)
    sweep(l2, vb2, va2, c2, g2, b2, 1, 2, 24, 0)
    for k in range(2):
        total = None
        for x0 in (l2.halo + 2 * k, l2.halo + 2 * k + 1):
            v, t = couple(l2, va2, c2, x0, 1, 8, 8)
            r = block(b2, 0, x0, 1, 8, 8) + t[0] - d2[pl.ds(x0 - l2.halo, 1), 0, :, :] * v[0]
            vc2[pl.ds(x0, 1), 0, pl.ds(8, 8), :] = v[0]
            total = r if total is None else total + r
        s2[pl.ds(8 * k, 8), :] = total[0]
    g_b3.send(tile_of(s2, 0.5))
    x_k2.send()
    f_k2.send()
    x_k0.forward()
    x_k1.forward()
    f_b2.forward()
    g_b3.forward()
    x_k2.forward()
    f_k2.forward()
    g_b3.finish()
    for k in range(l3.count):
        va3[l3.pad + k] = g3[k] * b3[l3.pad + k]
    packed_sweep(l3, va3, vb3, w3, wx3, g3, b3, l3.pad)
    packed_sweep(l3, vb3, va3, w3, wx3, g3, b3, l3.pad)

    def residual3(k):
        total = None
        for i in (2 * k, 2 * k + 1):
            v, t = packed_couple(l3, va3, w3, wx3, i)
            r = b3[pl.ds(l3.pad + i, 1)] + t - d3[pl.ds(i, 1)] * v
            total = r if total is None else total + r
        s3[pl.ds(k, 1), pl.ds(0, 8), :] = total
        s3[pl.ds(k, 1), pl.ds(8, 8), :] = total

    loop_pieces(nx, 2, residual3)
    res4[...] = packed_halve(s3, 0.5)

    sigma = THETA / DELTA
    rho = 1.0 / sigma
    for k in range(nx):
        direction = res4[k] * q4[k] * (1.0 / THETA)
        e4[k] = direction
        va4[l4.pad + k] = direction
    src, dst = va4, vb4
    for step in range(CHEB - 1):
        rho_new = 1.0 / (2.0 * sigma - rho)
        for k in range(nx):
            at = pl.ds(k, 1)
            v, t = packed_couple(l4, src, w4, wx4, k)
            r = res4[at] - (d4[at] * v - t)
            direction = (rho_new * rho) * v + (2.0 * rho_new / DELTA) * (r * q4[at])
            res4[at] = r
            e4[at] = e4[at] + direction
            dst[pl.ds(l4.pad + k, 1)] = direction
        rho = rho_new
        src, dst = dst, src

    row, col = iota((LANES, LANES), 0), iota((LANES, LANES), 1)
    spread = jnp.where(row == lax.shift_right_logical(col, 1), 1.0, 0.0).astype(F32)
    fine = dot(e4[...].reshape(nx * 8, LANES), spread).reshape(nx, 8, LANES)
    for dr in range(2):
        t3[:, pl.ds(dr, 4, stride=2), :] = fine[:, 0:4, :]
    for k in range(l3.count):
        vb3[l3.pad + k] = va3[l3.pad + k] + t3[k // 2]
    packed_sweep(l3, vb3, va3, w3, wx3, g3, b3, l3.pad)
    packed_sweep(l3, va3, vb3, w3, wx3, g3, b3, l3.pad)
    packed_sweep(l3, vb3, va3, w3, wx3, g3, b3, l3.pad)

    f_b2.finish()
    x_k2.finish()
    f_k2.finish()
    group = lax.shift_right_logical(gy, 1) - 1
    e3 = va3[pl.ds(l3.pad - 3 + 2 * gx, 8)].reshape(64, LANES)
    for q in range(3):
        pick = (row == lax.shift_right_logical(col, 1) + 32 * (group + q)) & (col < l2.nz)
        part = dot(e3, jnp.where(pick, 1.0, 0.0).astype(F32))
        pe2[:, 0, pl.ds(8 * q, 8), :] = part.reshape(8, 8, LANES)
    add_prolonged(l2, pe2, vc2, va2, 0, 0, 8, 16, 4 * (gy & 1) + 4)
    sweep(l2, va2, vb2, c2, g2, b2, 5, 2, 24, 0)
    sweep(l2, vb2, va2, c2, g2, b2, 4, 2, 24, 0)
    sweep(l2, va2, vb2, c2, g2, b2, 3, 2, 24, 0)

    x_k1.finish()
    prolong(l1, vb2, 3, 4, 10, 16, pe1, None, None, 0)
    add_prolonged(l1, pe1, vc1, va1, 0, 0, 10, 16)
    sweep(l1, va1, vb1, c1, g1, b1, 4, 4, 24, 0)
    sweep(l1, vb1, va1, c1, g1, b1, 3, 4, 24, 0)
    sweep(l1, va1, vb1, c1, g1, b1, 2, 4, 24, 0)

    x_k0.finish()
    prolong(l0, vb1, 4, 4, 12, 24, pe0, None, None, 0)
    add_prolonged(l0, pe0, vc0, va0, 0, 0, 12, 24)
    sweep(l0, va0, vb0, c0, g0, b0, 2, 4, 40, 2)
    sweep(l0, vb0, va0, c0, g0, b0, 1, 4, 40, 2)
    sweep(l0, va0, o0, c0, g0, b0, 0, 8, 32, 2, l0.halo, 8)
    stores = []
    for h in range(2):
        stores.append(
            pltpu.make_async_copy(
                o0.at[:, h], out.at[:, :, h * LANES : (h + 1) * LANES], local_sem.at[6 + h]
            )
        )
    for copy in stores:
        copy.start()
    for copy in stores:
        copy.wait()
    for exchange in list(everything):
        exchange.leave()
    g_c3.leave()
    g_b3.leave()


def solution(mesh):
    nx, ny = mesh.shape["gx"], mesh.shape["gy"]
    l0 = Level(2, 256, 4, 16, 32, 48, 16 * nx, 32 * ny)
    l1 = Level(1, 128, 6, 8, 16, 32, 8 * nx, 16 * ny)
    l2 = Level(1, 64, 6, 4, 8, 32, 4 * nx, 8 * ny)
    l3 = Packed(2 * nx, 4, 8, 32, ny // 2)
    l4 = Packed(nx, 1, 4, 16, ny // 2)

    def vmem(*shape):
        return pltpu.VMEM(shape, F32)

    e, o = (lambda l: l.ext()), (lambda l: l.own())
    scratch = [e(l0)] * 6 + [o(l0), vmem(8, 2, 32, LANES), o(l0), vmem(12, 2, 24, LANES)]
    scratch += [e(l1)] * 6 + [o(l1), vmem(4, 1, 16, LANES), vmem(10, 1, 16, LANES)]
    scratch += [e(l2)] * 6 + [o(l2), vmem(16, LANES), vmem(8, 1, 24, LANES)]
    scratch += [e(l3)] * 4 + [l3.own(1), o(l3), o(l3), vmem(nx, 16, LANES), vmem(nx, 8, LANES)]
    scratch += [o(l3)] * 4
    scratch += [e(l4)] * 3 + [l4.own(1)] + [o(l4)] * 8
    scratch += [vmem(ny, 8, LANES)] * 2
    copies = 10 * 8 + 3 * 6
    scratch += [
        pltpu.SemaphoreType.DMA((copies,)),
        pltpu.SemaphoreType.DMA((copies,)),
        pltpu.SemaphoreType.DMA((4,)),
        pltpu.SemaphoreType.DMA((4,)),
        pltpu.SemaphoreType.DMA((8,)),
    ]

    def step(guess, right_side, coefficient):
        return pl.pallas_call(
            functools.partial(kernel, nx, ny, (l0, l1, l2, l3, l4)),
            out_shape=jax.ShapeDtypeStruct(guess.shape, F32),
            in_specs=[pl.BlockSpec(memory_space=pl.ANY)] * 3,
            out_specs=pl.BlockSpec(memory_space=pl.ANY),
            scratch_shapes=scratch,
            compiler_params=pltpu.CompilerParams(collective_id=0, has_side_effects=True),
        )(guess, right_side, coefficient)

    spec = P("gx", "gy", None)
    return jax.shard_map(
        step, mesh=mesh, in_specs=(spec, spec, spec), out_specs=spec, check_vma=False
    )
```

time: 94.3 us -> 68.5 us (0.73)
  Pallas kernels: 92.3 us -> 66.3 us
    pallas_call x1, Pallas kernels: 92.3 us -> 66.3 us  [step(): pl.pallas_call(functools.partial(kernel, nx, ny, (l0, l1, l2, l3, l4)), o...]
where the time goes in v1:
time: 68.5 us; the launch traced here: 68.2 us
  Pallas kernels  66.3 us (97%)
  local copies, waits for them, and re-layouts  1.88 us (3%)
    pallas_call x1, Pallas kernels, step(): pl.pallas_call(functools.partial(kernel, nx, ny, (l0, l1, l2, l3, l4)), o...  66.3 us
    unnamed x1, local copies, waits for them, and re-layouts  1.88 us

profile of v1, /device:TPU:0, one launch (start us, length us, event | category | flops | bytes accessed | tf_op | source)
XLA Modules:
  0.0 68.2 jit_solution(9738919200339906002)
XLA Ops:
  0.0 66.3 %shard_map.37 = f32[16,32,256]{2,1,0:T(8,128)} custom-call(f32[16,32,256]{2,1,0:T(8,128)} %guess.1, f32[16,32,256]{2,1,0:T(8,128)} %rhs.1, f32[16,32,256]{2,1,0:T(8,128)} %coef.1), custom_call_target="tpu_custom_call" | custom-call | tf_op jit(solution)/shard_map/pallas_call | solution.py:753
  66.3 1.9 %copy.5 = f32[16,32,256]{2,1,0:T(8,128)} copy(f32[16,32,256]{2,1,0:T(8,128)} %shard_map.37) | data formatting | bytes 1048576

commit v2 on v1

--- a/solution.py
+++ b/solution.py
@@ -14,6 +14,7 @@
 THETA = 1.04
 DELTA = 0.96
 LANES = 128
+PIECES = 24
 
 
 def iota(shape, dim):
@@ -72,8 +73,8 @@
     return v, out
 
 
-def pieces(x0, count, r0, n):
-    return [(x0 + i, r0 + r) for i in range(count) for r in range(0, n, 8)]
+def tiles(r0, n):
+    return tuple(range(r0, r0 + n, 8))
 
 
 def loop(count, chunk, body):
@@ -85,72 +86,65 @@
         lax.fori_loop(0, steps, lambda k, _: (body(k * chunk), 0)[1], 0)
 
 
-def sweep(level, src, dst, c, g, b, rim, r0, n, chunk, dst_x=0, dst_r=0):
-    start = level.halo - rim
-    chunk = chunk or (level.bx + 2 * rim) // 2
-
-    def body(k):
-        for x0, r in pieces(start + k, chunk, r0, n):
-            v, t = couple(level, src, c, x0, 1, r, 8)
-            for h in range(level.nh):
-                new = (1.0 - RELAX) * v[h] + block(g, h, x0, 1, r, 8) * (
-                    t[h] + block(b, h, x0, 1, r, 8)
-                )
-                dst[pl.ds(x0 - dst_x, 1), h, pl.ds(r - dst_r, 8), :] = new
-
-    loop(level.bx + 2 * rim, chunk, body)
-
-
-def first_sweep(level, dst, g, b, rim, r0, n, chunk):
-    start = level.halo - rim
-    chunk = chunk or (level.bx + 2 * rim) // 2
-
-    def body(k):
-        x0 = start + k
+def over(level, span, rows, body):
+    lo, hi = span
+    most = max(1, (PIECES // level.nh) // len(rows))
+    chunk = max(c for c in range(1, hi - lo + 1) if (hi - lo) % c == 0 and c <= most)
+
+    def several(k):
+        for i in range(chunk):
+            for r in rows:
+                body(level.halo + lo + k + i, r)
+
+    loop(hi - lo, chunk, several)
+
+
+def sweep(level, src, dst, c, g, b, span, rows, put=None):
+    def body(x0, r):
+        v, t = couple(level, src, c, x0, 1, r, 8)
         for h in range(level.nh):
-            dst[pl.ds(x0, chunk), h, pl.ds(r0, n), :] = block(g, h, x0, chunk, r0, n) * block(
-                b, h, x0, chunk, r0, n
+            new = (1.0 - RELAX) * v[h] + block(g, h, x0, 1, r, 8) * (
+                t[h] + block(b, h, x0, 1, r, 8)
             )
-
-    loop(level.bx + 2 * rim, chunk, body)
-
-
-def setup(level, c, g, d, rim, r0, n, chunk, base_x, base_y, scale=RELAX):
-    start = level.halo - rim
-
-    def body(k):
+            if put is None:
+                dst[pl.ds(x0, 1), h, pl.ds(r, 8), :] = new
+            else:
+                put(x0, h, r, new)
+
+    over(level, span, rows, body)
+
+
+def first_sweep(level, dst, g, b, span, rows):
+    def body(x0, r):
+        for h in range(level.nh):
+            dst[pl.ds(x0, 1), h, pl.ds(r, 8), :] = block(g, h, x0, 1, r, 8) * block(
+                b, h, x0, 1, r, 8
+            )
+
+    over(level, span, rows, body)
+
+
+def setup(level, c, g, d, span, rows, base_x, base_y):
+    def body(x0, r):
         halves = range(level.nh)
-        for x0, r in pieces(start + k, chunk, r0, n):
-            mid = [block(c, h, x0, 1, r, 8) for h in halves]
-            cz = z_sum(level, mid)
-            shape = mid[0].shape
-            px = base_x + x0 - level.halo
-            py = iota(shape, 1) + jnp.where((px >= 0) & (px < level.total_x), base_y + r - 8, -1000)
-            mask = (py >= 0) & (py < level.total_y)
-            if level.nz < LANES:
-                mask = mask & (iota(shape, 2) < level.nz)
-            for h in halves:
-                total = 6.0 * mid[h] + cz[h]
-                for dx, dr in ((-1, 0), (1, 0), (0, -1), (0, 1)):
-                    total = total + block(c, h, x0 + dx, 1, r + dr, 8)
-                g[pl.ds(x0, 1), h, pl.ds(r, 8), :] = jnp.where(
-                    mask, scale / jnp.where(mask, total, 1.0), 0.0
-                )
-
-    loop(level.bx + 2 * rim, chunk, body)
-
-    def diagonal(k):
-        halves = range(level.nh)
-        for x0, r in pieces(level.halo + k, chunk, 8, level.by):
-            mid = [block(c, h, x0, 1, r, 8) for h in halves]
-            cz = z_sum(level, mid)
-            for h in halves:
-                total = 6.0 * mid[h] + cz[h]
-                for dx, dr in ((-1, 0), (1, 0), (0, -1), (0, 1)):
-                    total = total + block(c, h, x0 + dx, 1, r + dr, 8)
-                d[pl.ds(x0 - level.halo, 1), h, pl.ds(r - 8, 8), :] = total
-
-    loop(level.bx, chunk, diagonal)
+        mid = [block(c, h, x0, 1, r, 8) for h in halves]
+        cz = z_sum(level, mid)
+        shape = mid[0].shape
+        px = base_x + x0 - level.halo
+        py = iota(shape, 1) + jnp.where((px >= 0) & (px < level.total_x), base_y + r - 8, -1000)
+        mask = (py >= 0) & (py < level.total_y)
+        if level.nz < LANES:
+            mask = mask & (iota(shape, 2) < level.nz)
+        for h in halves:
+            total = 6.0 * mid[h] + cz[h]
+            for dx, dr in ((-1, 0), (1, 0), (0, -1), (0, 1)):
+                total = total + block(c, h, x0 + dx, 1, r + dr, 8)
+            g[pl.ds(x0, 1), h, pl.ds(r, 8), :] = jnp.where(
+                mask, RELAX / jnp.where(mask, total, 1.0), 0.0
+            )
+            d[pl.ds(x0, 1), h, pl.ds(r, 8), :] = total
+
+    over(level, span, rows, body)
 
 
 def residual_pairs(level, v_ref, c, b, d, s, keep):
@@ -161,7 +155,7 @@
                 x0 = level.halo + 2 * k + dx
                 v, t = couple(level, v_ref, c, x0, 1, 8 + r, 8)
                 for h in range(level.nh):
-                    own = d[pl.ds(2 * k + dx, 1), h, pl.ds(r, 8), :]
+                    own = block(d, h, x0, 1, 8 + r, 8)
                     parts.append(block(b, h, x0, 1, 8 + r, 8) + t[h] - own * v[h])
                     if keep is not None:
                         keep[pl.ds(x0, 1), h, pl.ds(8 + r, 8), :] = v[h]
@@ -328,7 +322,7 @@
     l0, l1, l2, l3, l4 = levels
     names = iter(scratch)
     take = lambda k: [next(names) for _ in range(k)]
-    va0, vb0, vc0, c0, b0, g0, d0, s0, o0, pe0 = take(10)
+    va0, vb0, vc0, c0, b0, g0, d0, ve0, vf0, s0, pe0 = take(11)
     va1, vb1, vc1, c1, b1, g1, d1, s1, pe1 = take(9)
     va2, vb2, vc2, c2, b2, g2, d2, s2, pe2 = take(9)
     va3, vb3, c3, b3, wx3, g3, d3, s3, t3 = take(9)
@@ -367,10 +361,16 @@
             barrier, inc=1, device_id=(gx, lax.rem(gy + k, ny)), device_id_type=MESH
         )
 
+    for dx in (1, nx - 1):
+        for dy in (1, ny - 1):
+            diagonal = (lax.rem(gx + dx, nx), lax.rem(gy + dy, ny))
+            pl.semaphore_signal(barrier, inc=1, device_id=diagonal, device_id_type=MESH)
+
     everything = []
 
     class Exchange:
-        def __init__(self, level, ref, wide, reach=1, faces=True):
+        def __init__(self, level, ref, wide, reach=1, faces=True, direct=False):
+            self.direct = direct
             lo, bx, by = level.halo, level.bx, level.by
             if reach == 1:
                 up = ((lo + bx - wide, lo - wide), (lo, lo + bx))
@@ -393,35 +393,48 @@
                 )
             rows = 4 if level.nh == 2 else 8
             sides = ((1, 8 + by - rows, 8 - rows), (-1, 8, 8 + by))
+            inside_x, inside_y = (lambda p: (p >= 0) & (p < nx)), (lambda p: (p >= 0) & (p < ny))
             for sign, src, dst in sides:
                 there, back = gy + sign, gy - sign
-                ok_y = lambda p: (p >= 0) & (p < ny)
-                spans = [(lo, bx, None)] if faces else []
-                spans += [(up[0][1], wide, gx - reach >= 0), (up[1][1], wide, gx + reach < nx)]
-                for start, count, also in spans:
-                    sends, receives = ok_y(there), ok_y(back)
-                    if also is not None:
-                        sends, receives = sends & also, receives & also
-                    (self.y if also is None else self.corners).append(
+                sends, receives = inside_y(there), inside_y(back)
+
+                def strip(start, count, row):
+                    return ref.at[pl.ds(start, count), :, pl.ds(row, rows), :]
+
+                if faces:
+                    self.y.append(
                         Copy(
-                            ref.at[pl.ds(start, count), :, pl.ds(src, rows), :],
-                            ref.at[pl.ds(start, count), :, pl.ds(dst, rows), :],
+                            strip(lo, bx, src),
+                            strip(lo, bx, dst),
                             (gx, there),
                             sends,
                             receives,
                             sems(),
                         )
                     )
+                for sign_x, (src_x, dst_x) in zip((1, -1), up):
+                    far, near = gx + sign_x * reach, gx - sign_x * reach
+                    have = receives & inside_x(near)
+                    self.corners.append(
+                        Copy(
+                            strip(src_x if direct else dst_x, wide, src),
+                            strip(dst_x, wide, dst),
+                            (far if direct else gx, there),
+                            sends & inside_x(far if direct else near),
+                            have,
+                            sems(),
+                        )
+                    )
             everything.append(self)
 
         def send(self):
-            for copy in self.x + self.y:
+            for copy in self.x + self.y + (self.corners if self.direct else []):
                 copy.start()
 
         def forward(self):
             for copy in self.x:
                 copy.arrive()
-            for copy in self.corners:
+            for copy in [] if self.direct else self.corners:
                 copy.start()
 
         def finish(self):
@@ -485,14 +498,15 @@
 
     x_v0, x_c0, x_b0 = Exchange(l0, va0, 4), Exchange(l0, c0, 4), Exchange(l0, b0, 3)
     x_k0 = Exchange(l0, vc0, 3)
-    x_c1, x_b1, x_k1 = Exchange(l1, c1, 5), Exchange(l1, b1, 4), Exchange(l1, vc1, 5)
-    x_c2, x_b2, x_k2 = (Exchange(l2, ref, 4) for ref in (c2, b2, vc2))
+    x_c1, x_b1, x_k1 = Exchange(l1, c1, 5), Exchange(l1, b1, 4, direct=True), Exchange(l1, vc1, 5)
+    x_c2, x_k2 = Exchange(l2, c2, 4), Exchange(l2, vc2, 4)
+    x_b2 = Exchange(l2, b2, 4, direct=True)
     f_c2, f_b2, f_k2 = (Exchange(l2, ref, 2, 2, False) for ref in (c2, b2, vc2))
     g_c3, g_b3 = Gather(pc, c3, l3.pad, 0), Gather(pb, b3, l3.pad, 2)
 
     for copy in loads:
         copy.wait()
-    pl.semaphore_wait(barrier, nx + ny - 2)
+    pl.semaphore_wait(barrier, nx + ny + 2)
 
     x_c0.send()
     x_v0.send()
@@ -534,7 +548,7 @@
         pad = 1 if ref.shape[0] == nx + 2 else l3.pad
         for start in (0, ref.shape[0] - pad):
             ref[pl.ds(start, pad)] = jnp.zeros((pad, 8, LANES), F32)
-    for ref in (vb0, va1, vb1, va2, vb2):
+    for ref in (va1, vb1, va2, vb2):
         for h in range(ref.shape[1]):
             for r in range(0, ref.shape[2], 8):
                 ref[:, h, pl.ds(r, 8), :] = jnp.zeros((ref.shape[0], 8, LANES), F32)
@@ -561,33 +575,43 @@
         )
     g_c3.send(tile_of(s2, 0.125))
 
-    for exchange in (x_c0, x_v0, x_b0):
-        exchange.forward()
+    bx0, by0 = gx * l0.bx, gy * l0.by
+    chain = (va0, vb0, ve0, vf0)
+    inner = tiles(12, 24)
+    setup(l0, c0, g0, d0, (1, l0.bx - 1), inner, bx0, by0)
+    for k in range(1, 4):
+        sweep(l0, chain[k - 1], chain[k], c0, g0, b0, (k, l0.bx - k), inner)
+    x_c0.forward()
+    for span in ((-3, 1), (l0.bx - 1, l0.bx + 3)):
+        setup(l0, c0, g0, d0, span, inner, bx0, by0)
+    x_v0.forward()
+    x_b0.forward()
+    for k in range(1, 4):
+        for span in ((k - 4, k), (l0.bx - k, l0.bx + 4 - k)):
+            sweep(l0, chain[k - 1], chain[k], c0, g0, b0, span, inner)
     for exchange in (x_c0, x_v0, x_b0):
         exchange.finish()
     g_c3.forward()
     for exchange in (x_c1, x_c2, f_c2):
         exchange.forward()
-    bx0, by0 = gx * l0.bx, gy * l0.by
-
-    setup(l0, c0, g0, d0, 3, 4, 40, 2, bx0, by0)
-    sweep(l0, va0, vb0, c0, g0, b0, 3, 4, 40, 2)
-    x_v0.leave()
-    sweep(l0, vb0, va0, c0, g0, b0, 2, 4, 40, 2)
-    sweep(l0, va0, vb0, c0, g0, b0, 1, 4, 40, 2)
-    residual_pairs(l0, vb0, c0, b0, d0, s0, vc0)
+    setup(l0, c0, g0, d0, (-3, l0.bx + 3), (4, 36), bx0, by0)
+    for k in range(1, 4):
+        span = (k - 4, l0.bx + 4 - k)
+        sweep(l0, chain[k - 1], chain[k], c0, g0, b0, span, (3 + k, 37 - k))
+    residual_pairs(l0, vf0, c0, b0, d0, s0, vc0)
     b1[l1.halo : l1.halo + l1.bx, 0, 8 : 8 + l1.by, :] = halve(l0, s0, 0.5)
     x_b1.send()
     x_k0.send()
     for exchange in (x_c1, x_c2, f_c2):
         exchange.finish()
-    setup(l1, c1, g1, d1, 4, 4, 24, 2, gx * l1.bx, gy * l1.by)
-    setup(l2, c2, g2, d2, 5, 2, 24, 2, gx * l2.bx, gy * l2.by)
+    rows1, rows2 = tiles(4, 24), tiles(2, 24)
+    setup(l1, c1, g1, d1, (-4, l1.bx + 4), rows1, gx * l1.bx, gy * l1.by)
+    setup(l2, c2, g2, d2, (-5, l2.bx + 5), rows2, gx * l2.bx, gy * l2.by)
     x_b1.forward()
     x_b1.finish()
-    first_sweep(l1, va1, g1, b1, 3, 4, 24, 0)
-    sweep(l1, va1, vb1, c1, g1, b1, 2, 4, 24, 0)
-    sweep(l1, vb1, va1, c1, g1, b1, 1, 4, 24, 0)
+    first_sweep(l1, va1, g1, b1, (-3, l1.bx + 3), rows1)
+    sweep(l1, va1, vb1, c1, g1, b1, (-2, l1.bx + 2), rows1)
+    sweep(l1, vb1, va1, c1, g1, b1, (-1, l1.bx + 1), rows1)
     residual_pairs(l1, va1, c1, b1, d1, s1, vc1)
     b2[l2.halo : l2.halo + l2.bx, 0, 8 : 8 + l2.by, :] = halve(l1, s1, 0.5)
     x_b2.send()
@@ -608,14 +632,14 @@
 
     x_b2.forward()
     x_b2.finish()
-    first_sweep(l2, va2, g2, b2, 3, 2, 24, 0)
-    sweep(l2, va2, vb2, c2, g2, b2, 2, 2, 24, 0)
-    sweep(l2, vb2, va2, c2, g2, b2, 1, 2, 24, 0)
+    first_sweep(l2, va2, g2, b2, (-3, l2.bx + 3), rows2)
+    sweep(l2, va2, vb2, c2, g2, b2, (-2, l2.bx + 2), rows2)
+    sweep(l2, vb2, va2, c2, g2, b2, (-1, l2.bx + 1), rows2)
     for k in range(2):
         total = None
         for x0 in (l2.halo + 2 * k, l2.halo + 2 * k + 1):
             v, t = couple(l2, va2, c2, x0, 1, 8, 8)
-            r = block(b2, 0, x0, 1, 8, 8) + t[0] - d2[pl.ds(x0 - l2.halo, 1), 0, :, :] * v[0]
+            r = block(b2, 0, x0, 1, 8, 8) + t[0] - block(d2, 0, x0, 1, 8, 8) * v[0]
             vc2[pl.ds(x0, 1), 0, pl.ds(8, 8), :] = v[0]
             total = r if total is None else total + r
         s2[pl.ds(8 * k, 8), :] = total[0]
@@ -687,34 +711,27 @@
         part = dot(e3, jnp.where(pick, 1.0, 0.0).astype(F32))
         pe2[:, 0, pl.ds(8 * q, 8), :] = part.reshape(8, 8, LANES)
     add_prolonged(l2, pe2, vc2, va2, 0, 0, 8, 16, 4 * (gy & 1) + 4)
-    sweep(l2, va2, vb2, c2, g2, b2, 5, 2, 24, 0)
-    sweep(l2, vb2, va2, c2, g2, b2, 4, 2, 24, 0)
-    sweep(l2, va2, vb2, c2, g2, b2, 3, 2, 24, 0)
+    sweep(l2, va2, vb2, c2, g2, b2, (-5, l2.bx + 5), rows2)
+    sweep(l2, vb2, va2, c2, g2, b2, (-4, l2.bx + 4), rows2)
+    sweep(l2, va2, vb2, c2, g2, b2, (-3, l2.bx + 3), rows2)
 
     x_k1.finish()
     prolong(l1, vb2, 3, 4, 10, 16, pe1, None, None, 0)
     add_prolonged(l1, pe1, vc1, va1, 0, 0, 10, 16)
-    sweep(l1, va1, vb1, c1, g1, b1, 4, 4, 24, 0)
-    sweep(l1, vb1, va1, c1, g1, b1, 3, 4, 24, 0)
-    sweep(l1, va1, vb1, c1, g1, b1, 2, 4, 24, 0)
+    sweep(l1, va1, vb1, c1, g1, b1, (-4, l1.bx + 4), rows1)
+    sweep(l1, vb1, va1, c1, g1, b1, (-3, l1.bx + 3), rows1)
+    sweep(l1, va1, vb1, c1, g1, b1, (-2, l1.bx + 2), rows1)
 
     x_k0.finish()
     prolong(l0, vb1, 4, 4, 12, 24, pe0, None, None, 0)
+    x_v0.leave()
     add_prolonged(l0, pe0, vc0, va0, 0, 0, 12, 24)
-    sweep(l0, va0, vb0, c0, g0, b0, 2, 4, 40, 2)
-    sweep(l0, vb0, va0, c0, g0, b0, 1, 4, 40, 2)
-    sweep(l0, va0, o0, c0, g0, b0, 0, 8, 32, 2, l0.halo, 8)
-    stores = []
-    for h in range(2):
-        stores.append(
-            pltpu.make_async_copy(
-                o0.at[:, h], out.at[:, :, h * LANES : (h + 1) * LANES], local_sem.at[6 + h]
-            )
-        )
-    for copy in stores:
-        copy.start()
-    for copy in stores:
-        copy.wait()
+    def put(x0, h, r, new):
+        out[pl.ds(x0 - l0.halo, 1), pl.ds(r - 8, 8), h * LANES : (h + 1) * LANES] = new
+
+    sweep(l0, va0, vb0, c0, g0, b0, (-2, l0.bx + 2), tiles(4, 40))
+    sweep(l0, vb0, ve0, c0, g0, b0, (-1, l0.bx + 1), tiles(4, 40))
+    sweep(l0, ve0, None, c0, g0, b0, (0, l0.bx), tiles(8, 32), put)
     for exchange in list(everything):
         exchange.leave()
     g_c3.leave()
@@ -733,9 +750,9 @@
         return pltpu.VMEM(shape, F32)
 
     e, o = (lambda l: l.ext()), (lambda l: l.own())
-    scratch = [e(l0)] * 6 + [o(l0), vmem(8, 2, 32, LANES), o(l0), vmem(12, 2, 24, LANES)]
-    scratch += [e(l1)] * 6 + [o(l1), vmem(4, 1, 16, LANES), vmem(10, 1, 16, LANES)]
-    scratch += [e(l2)] * 6 + [o(l2), vmem(16, LANES), vmem(8, 1, 24, LANES)]
+    scratch = [e(l0)] * 9 + [vmem(8, 2, 32, LANES), vmem(12, 2, 24, LANES)]
+    scratch += [e(l1)] * 7 + [vmem(4, 1, 16, LANES), vmem(10, 1, 16, LANES)]
+    scratch += [e(l2)] * 7 + [vmem(16, LANES), vmem(8, 1, 24, LANES)]
     scratch += [e(l3)] * 4 + [l3.own(1), o(l3), o(l3), vmem(nx, 16, LANES), vmem(nx, 8, LANES)]
     scratch += [o(l3)] * 4
     scratch += [e(l4)] * 3 + [l4.own(1)] + [o(l4)] * 8
@@ -752,9 +769,9 @@
     def step(guess, right_side, coefficient):
         return pl.pallas_call(
             functools.partial(kernel, nx, ny, (l0, l1, l2, l3, l4)),
-            out_shape=jax.ShapeDtypeStruct(guess.shape, F32),
+            out_shape=pltpu.VMEM(guess.shape, F32),
             in_specs=[pl.BlockSpec(memory_space=pl.ANY)] * 3,
-            out_specs=pl.BlockSpec(memory_space=pl.ANY),
+            out_specs=pl.BlockSpec(memory_space=pltpu.VMEM),
             scratch_shapes=scratch,
             compiler_params=pltpu.CompilerParams(collective_id=0, has_side_effects=True),
         )(guess, right_side, coefficient)

time: 68.5 us -> 59.8 us (0.87)
  Pallas kernels: 66.3 us -> 58.9 us
  local copies, waits for them, and re-layouts: 1.88 us -> 0.8 us
    pallas_call x1, Pallas kernels: 66.3 us -> 58.9 us  [step(): pl.pallas_call(functools.partial(kernel, nx, ny, (l0, l1, l2, l3, l4)), o...]
    unnamed x1, local copies, waits for them, and re-layouts: 1.88 us -> 0.8 us
where the time goes in v2:
time: 59.8 us; the launch traced here: 59.7 us
  Pallas kernels  58.9 us (98%)
  local copies, waits for them, and re-layouts  0.8 us (1%)
    pallas_call x1, Pallas kernels, step(): pl.pallas_call(functools.partial(kernel, nx, ny, (l0, l1, l2, l3, l4)), o...  58.9 us

profile of v2, /device:TPU:0, one launch (start us, length us, event | category | flops | bytes accessed | tf_op | source)
XLA Modules:
  0.0 59.7 jit_solution(15190629058537378823)
XLA Ops:
  0.0 58.9 %shard_map.37 = f32[16,32,256]{2,1,0:T(8,128)S(1)} custom-call(f32[16,32,256]{2,1,0:T(8,128)} %guess.1, f32[16,32,256]{2,1,0:T(8,128)} %rhs.1, f32[16,32,256]{2,1,0:T(8,128)} %coef.1), custom_call_target="tpu_custom_call" | custom-call | tf_op jit(solution)/shard_map/pallas_call | solution.py:770
  58.9 0.8 %copy.5 = f32[16,32,256]{2,1,0:T(8,128)} copy(f32[16,32,256]{2,1,0:T(8,128)S(1)} %shard_map.37) | data formatting | bytes 1048576

commit v3 on v2

--- a/solution.py
+++ b/solution.py
@@ -14,7 +14,7 @@
 THETA = 1.04
 DELTA = 0.96
 LANES = 128
-PIECES = 24
+REGISTERS = 120
 
 
 def iota(shape, dim):
@@ -35,46 +35,33 @@
 
 
 def z_sum(level, v):
-    lane = iota(v[0].shape, 2)
-    up = [pltpu.roll(a, 1, 2) for a in v]
-    down = [pltpu.roll(a, LANES - 1, 2) for a in v]
-    if level.nh == 2:
-        low = [jnp.where(lane == 0, 0.0, up[0]), jnp.where(lane == 0, up[0], up[1])]
-        high = [
-            jnp.where(lane == LANES - 1, down[1], down[0]),
-            jnp.where(lane == LANES - 1, 0.0, down[1]),
-        ]
-    elif level.nz == LANES:
-        low = [jnp.where(lane == 0, 0.0, up[0])]
-        high = [jnp.where(lane == LANES - 1, 0.0, down[0])]
-    else:
-        low, high = up, down
-    return [a + b for a, b in zip(low, high)]
-
-
-def block(ref, half, x0, cx, r0, n):
-    return ref[pl.ds(x0, cx), half, pl.ds(r0, n), :]
-
-
-def couple(level, v_ref, c_ref, x0, cx, r0, n):
-    halves = range(level.nh)
-    v = [block(v_ref, h, x0, cx, r0, n) for h in halves]
-    c = [block(c_ref, h, x0, cx, r0, n) for h in halves]
-    vz = z_sum(level, v)
-    uz = z_sum(level, [a * b for a, b in zip(c, v)])
-    out = []
-    for h in halves:
-        sv, su = vz[h], uz[h]
-        for dx, dr in ((-1, 0), (1, 0), (0, -1), (0, 1)):
-            near = block(v_ref, h, x0 + dx, cx, r0 + dr, n)
-            sv = sv + near
-            su = su + near * block(c_ref, h, x0 + dx, cx, r0 + dr, n)
-        out.append(c[h] * sv + su)
-    return v, out
-
-
-def tiles(r0, n):
-    return tuple(range(r0, r0 + n, 8))
+    lane = iota(v.shape, 3)
+    up, down = pltpu.roll(v, 1, 3), pltpu.roll(v, LANES - 1, 3)
+    if level.nz >= LANES:
+        none = jnp.zeros_like(v[:, :1])
+        below = jnp.concatenate([none, up[:, :1]], 1) if level.nh == 2 else none
+        above = jnp.concatenate([down[:, 1:], none], 1) if level.nh == 2 else none
+        up = jnp.where(lane == 0, below, up)
+        down = jnp.where(lane == LANES - 1, above, down)
+    return up + down
+
+
+def block(ref, x0, r0, n):
+    return ref[pl.ds(x0, 1), :, pl.ds(r0, n), :]
+
+
+def couple(level, v_ref, c_ref, x0, r0, n):
+    v, c = block(v_ref, x0, r0, n), block(c_ref, x0, r0, n)
+    sv, su = z_sum(level, v), z_sum(level, c * v)
+    for dx, dr in ((-1, 0), (1, 0), (0, -1), (0, 1)):
+        near = block(v_ref, x0 + dx, r0 + dr, n)
+        sv = sv + near
+        su = su + near * block(c_ref, x0 + dx, r0 + dr, n)
+    return v, c * sv + su
+
+
+def tiles(r0, n, most=16):
+    return tuple((r, min(most, r0 + n - r)) for r in range(r0, r0 + n, most))
 
 
 def loop(count, chunk, body):
@@ -88,92 +75,78 @@
 
 def over(level, span, rows, body):
     lo, hi = span
-    most = max(1, (PIECES // level.nh) // len(rows))
+    each = level.nh * sum(n for _, n in rows) // 8
+    most = max(1, REGISTERS // each)
     chunk = max(c for c in range(1, hi - lo + 1) if (hi - lo) % c == 0 and c <= most)
 
     def several(k):
         for i in range(chunk):
-            for r in rows:
-                body(level.halo + lo + k + i, r)
+            for r, n in rows:
+                body(level.halo + lo + k + i, r, n)
 
     loop(hi - lo, chunk, several)
 
 
 def sweep(level, src, dst, c, g, b, span, rows, put=None):
-    def body(x0, r):
-        v, t = couple(level, src, c, x0, 1, r, 8)
-        for h in range(level.nh):
-            new = (1.0 - RELAX) * v[h] + block(g, h, x0, 1, r, 8) * (
-                t[h] + block(b, h, x0, 1, r, 8)
-            )
-            if put is None:
-                dst[pl.ds(x0, 1), h, pl.ds(r, 8), :] = new
-            else:
-                put(x0, h, r, new)
+    def body(x0, r, n):
+        v, t = couple(level, src, c, x0, r, n)
+        new = (1.0 - RELAX) * v + block(g, x0, r, n) * (t + block(b, x0, r, n))
+        if put is None:
+            dst[pl.ds(x0, 1), :, pl.ds(r, n), :] = new
+        else:
+            put(x0, r, n, new)
 
     over(level, span, rows, body)
 
 
 def first_sweep(level, dst, g, b, span, rows):
-    def body(x0, r):
-        for h in range(level.nh):
-            dst[pl.ds(x0, 1), h, pl.ds(r, 8), :] = block(g, h, x0, 1, r, 8) * block(
-                b, h, x0, 1, r, 8
-            )
+    def body(x0, r, n):
+        dst[pl.ds(x0, 1), :, pl.ds(r, n), :] = block(g, x0, r, n) * block(b, x0, r, n)
 
     over(level, span, rows, body)
 
 
 def setup(level, c, g, d, span, rows, base_x, base_y):
-    def body(x0, r):
-        halves = range(level.nh)
-        mid = [block(c, h, x0, 1, r, 8) for h in halves]
-        cz = z_sum(level, mid)
-        shape = mid[0].shape
+    def body(x0, r, n):
+        mid = block(c, x0, r, n)
         px = base_x + x0 - level.halo
-        py = iota(shape, 1) + jnp.where((px >= 0) & (px < level.total_x), base_y + r - 8, -1000)
+        py = iota(mid.shape, 2) + jnp.where(
+            (px >= 0) & (px < level.total_x), base_y + r - 8, -1000
+        )
         mask = (py >= 0) & (py < level.total_y)
         if level.nz < LANES:
-            mask = mask & (iota(shape, 2) < level.nz)
-        for h in halves:
-            total = 6.0 * mid[h] + cz[h]
-            for dx, dr in ((-1, 0), (1, 0), (0, -1), (0, 1)):
-                total = total + block(c, h, x0 + dx, 1, r + dr, 8)
-            g[pl.ds(x0, 1), h, pl.ds(r, 8), :] = jnp.where(
-                mask, RELAX / jnp.where(mask, total, 1.0), 0.0
-            )
-            d[pl.ds(x0, 1), h, pl.ds(r, 8), :] = total
+            mask = mask & (iota(mid.shape, 3) < level.nz)
+        total = 6.0 * mid + z_sum(level, mid)
+        for dx, dr in ((-1, 0), (1, 0), (0, -1), (0, 1)):
+            total = total + block(c, x0 + dx, r + dr, n)
+        g[pl.ds(x0, 1), :, pl.ds(r, n), :] = jnp.where(
+            mask, RELAX / jnp.where(mask, total, 1.0), 0.0
+        )
+        d[pl.ds(x0, 1), :, pl.ds(r, n), :] = total
 
     over(level, span, rows, body)
 
 
 def residual_pairs(level, v_ref, c, b, d, s, keep):
     def body(k):
-        for r in range(0, level.by, 8):
-            parts = []
-            for dx in range(2):
-                x0 = level.halo + 2 * k + dx
-                v, t = couple(level, v_ref, c, x0, 1, 8 + r, 8)
-                for h in range(level.nh):
-                    own = block(d, h, x0, 1, 8 + r, 8)
-                    parts.append(block(b, h, x0, 1, 8 + r, 8) + t[h] - own * v[h])
-                    if keep is not None:
-                        keep[pl.ds(x0, 1), h, pl.ds(8 + r, 8), :] = v[h]
-            for h in range(level.nh):
-                total = parts[h] + parts[level.nh + h]
-                s[pl.ds(k, 1), h, pl.ds(r, 8), :] = total
-
-    loop(level.bx // 2, 1, body)
+        for r, n in tiles(8, level.by):
+            total = None
+            for x0 in (level.halo + 2 * k, level.halo + 2 * k + 1):
+                v, t = couple(level, v_ref, c, x0, r, n)
+                part = block(b, x0, r, n) + t - block(d, x0, r, n) * v
+                keep[pl.ds(x0, 1), :, pl.ds(r, n), :] = v
+                total = part if total is None else total + part
+            s[pl.ds(k, 1), :, pl.ds(r - 8, n), :] = total
+
+    loop_pieces(level.bx // 2, 4, body)
 
 
 def field_pairs(level, ref, s):
     def body(k):
         x0 = level.halo + 2 * k
-        for h in range(level.nh):
-            r = block(ref, h, x0, 1, 8, level.by) + block(ref, h, x0 + 1, 1, 8, level.by)
-            s[pl.ds(k, 1), h, pl.ds(0, level.by), :] = r
-
-    loop(level.bx // 2, 1, body)
+        s[pl.ds(k, 1)] = block(ref, x0, 8, level.by) + block(ref, x0 + 1, 8, level.by)
+
+    loop_pieces(level.bx // 2, 4, body)
 
 
 def dot(a, m):
@@ -516,7 +489,7 @@
             own = (pl.ds(l0.halo + k, 1), h, pl.ds(8, l0.by), slice(None))
             b0[own] = 2.0 * b0[own]
 
-    loop(l0.bx, 1, double)
+    loop_pieces(l0.bx, 4, double)
     x_b0.send()
 
     def clear(level, refs, far):
@@ -594,17 +567,17 @@
     g_c3.forward()
     for exchange in (x_c1, x_c2, f_c2):
         exchange.forward()
-    setup(l0, c0, g0, d0, (-3, l0.bx + 3), (4, 36), bx0, by0)
+    setup(l0, c0, g0, d0, (-3, l0.bx + 3), ((4, 8), (36, 8)), bx0, by0)
     for k in range(1, 4):
         span = (k - 4, l0.bx + 4 - k)
-        sweep(l0, chain[k - 1], chain[k], c0, g0, b0, span, (3 + k, 37 - k))
+        sweep(l0, chain[k - 1], chain[k], c0, g0, b0, span, ((3 + k, 8), (37 - k, 8)))
     residual_pairs(l0, vf0, c0, b0, d0, s0, vc0)
     b1[l1.halo : l1.halo + l1.bx, 0, 8 : 8 + l1.by, :] = halve(l0, s0, 0.5)
     x_b1.send()
     x_k0.send()
     for exchange in (x_c1, x_c2, f_c2):
         exchange.finish()
-    rows1, rows2 = tiles(4, 24), tiles(2, 24)
+    rows1, rows2 = tiles(4, 24, 24), tiles(2, 24, 24)
     setup(l1, c1, g1, d1, (-4, l1.bx + 4), rows1, gx * l1.bx, gy * l1.by)
     setup(l2, c2, g2, d2, (-5, l2.bx + 5), rows2, gx * l2.bx, gy * l2.by)
     x_b1.forward()
@@ -638,11 +611,11 @@
     for k in range(2):
         total = None
         for x0 in (l2.halo + 2 * k, l2.halo + 2 * k + 1):
-            v, t = couple(l2, va2, c2, x0, 1, 8, 8)
-            r = block(b2, 0, x0, 1, 8, 8) + t[0] - block(d2, 0, x0, 1, 8, 8) * v[0]
-            vc2[pl.ds(x0, 1), 0, pl.ds(8, 8), :] = v[0]
-            total = r if total is None else total + r
-        s2[pl.ds(8 * k, 8), :] = total[0]
+            v, t = couple(l2, va2, c2, x0, 8, 8)
+            part = block(b2, x0, 8, 8) + t - block(d2, x0, 8, 8) * v
+            vc2[pl.ds(x0, 1), :, pl.ds(8, 8), :] = v
+            total = part if total is None else total + part
+        s2[pl.ds(8 * k, 8), :] = total[0, 0]
     g_b3.send(tile_of(s2, 0.5))
     x_k2.send()
     f_k2.send()
@@ -726,8 +699,10 @@
     prolong(l0, vb1, 4, 4, 12, 24, pe0, None, None, 0)
     x_v0.leave()
     add_prolonged(l0, pe0, vc0, va0, 0, 0, 12, 24)
-    def put(x0, h, r, new):
-        out[pl.ds(x0 - l0.halo, 1), pl.ds(r - 8, 8), h * LANES : (h + 1) * LANES] = new
+    def put(x0, r, n, new):
+        for h in range(2):
+            at = (pl.ds(x0 - l0.halo, 1), pl.ds(r - 8, n), slice(h * LANES, (h + 1) * LANES))
+            out[at] = new[:, h]
 
     sweep(l0, va0, vb0, c0, g0, b0, (-2, l0.bx + 2), tiles(4, 40))
     sweep(l0, vb0, ve0, c0, g0, b0, (-1, l0.bx + 1), tiles(4, 40))

time: 59.8 us -> 54.1 us (0.905)
  Pallas kernels: 58.9 us -> 53.2 us
    pallas_call x1, Pallas kernels: 58.9 us -> 53.2 us  [step(): pl.pallas_call(functools.partial(kernel, nx, ny, (l0, l1, l2, l3, l4)), o...]
where the time goes in v3:
time: 54.1 us; the launch traced here: 54 us
  Pallas kernels  53.2 us (98%)
  local copies, waits for them, and re-layouts  0.8 us (1%)
    pallas_call x1, Pallas kernels, step(): pl.pallas_call(functools.partial(kernel, nx, ny, (l0, l1, l2, l3, l4)), o...  53.2 us

profile of v3, /device:TPU:0, one launch (start us, length us, event | category | flops | bytes accessed | tf_op | source)
XLA Modules:
  0.0 54.0 jit_solution(8405999066386463351)
XLA Ops:
  0.0 53.2 %shard_map.37 = f32[16,32,256]{2,1,0:T(8,128)S(1)} custom-call(f32[16,32,256]{2,1,0:T(8,128)} %guess.1, f32[16,32,256]{2,1,0:T(8,128)} %rhs.1, f32[16,32,256]{2,1,0:T(8,128)} %coef.1), custom_call_target="tpu_custom_call" | custom-call | tf_op jit(solution)/shard_map/pallas_call | solution.py:745
  53.2 0.8 %copy.5 = f32[16,32,256]{2,1,0:T(8,128)} copy(f32[16,32,256]{2,1,0:T(8,128)S(1)} %shard_map.37) | data formatting | bytes 1048576

commit v4 on v3

--- a/solution.py
+++ b/solution.py
@@ -127,8 +127,11 @@
     over(level, span, rows, body)
 
 
-def residual_pairs(level, v_ref, c, b, d, s, keep):
-    def body(k):
+def residual_pairs(level, v_ref, c, b, d, s, keep, span=None):
+    lo, hi = span or (0, level.bx // 2)
+
+    def body(i):
+        k = lo + i
         for r, n in tiles(8, level.by):
             total = None
             for x0 in (level.halo + 2 * k, level.halo + 2 * k + 1):
@@ -138,7 +141,8 @@
                 total = part if total is None else total + part
             s[pl.ds(k, 1), :, pl.ds(r - 8, n), :] = total
 
-    loop_pieces(level.bx // 2, 4, body)
+    count = hi - lo
+    loop_pieces(count, max(i for i in (1, 2, 3, 4) if count % i == 0), body)
 
 
 def field_pairs(level, ref, s):
@@ -268,27 +272,37 @@
     return dot(a.reshape(s.shape[0] * 8, LANES), m).reshape(s.shape[0], 8, LANES)
 
 
-class Copy:
-    def __init__(self, src, dst, target, sends, receives, sems):
+class Bundle:
+    def __init__(self, pairs, target, sends, receives, tiles, unit, sems):
         send_sem, recv_sem, index = sems
-        self.copy = pltpu.make_async_remote_copy(
-            src_ref=src,
-            dst_ref=dst,
-            send_sem=send_sem.at[index],
-            recv_sem=recv_sem.at[index],
-            device_id=target,
-            device_id_type=MESH,
-        )
+
+        def copy(src, dst):
+            return pltpu.make_async_remote_copy(
+                src_ref=src,
+                dst_ref=dst,
+                send_sem=send_sem.at[index],
+                recv_sem=recv_sem.at[index],
+                device_id=target,
+                device_id_type=MESH,
+            )
+
+        self.copies = [copy(src, dst) for src, dst in pairs]
+        whole = unit.at[pl.ds(0, tiles)]
+        self.whole = self.copies[0] if len(pairs) == 1 else copy(whole, whole)
         self.sends, self.receives = sends, receives
 
     def start(self):
-        pl.when(self.sends)(lambda: self.copy.start())
+        def go():
+            for copy in self.copies:
+                copy.start()
+
+        pl.when(self.sends)(go)
 
     def arrive(self):
-        pl.when(self.receives)(lambda: self.copy.wait_recv())
+        pl.when(self.receives)(lambda: self.whole.wait_recv())
 
     def leave(self):
-        pl.when(self.sends)(lambda: self.copy.wait_send())
+        pl.when(self.sends)(lambda: self.whole.wait_send())
 
 
 def kernel(nx, ny, levels, guess, rhs, coef, out, *scratch):
@@ -302,7 +316,7 @@
     w3 = take(4)
     va4, vb4, c4, wx4, q4, d4, res4, e4 = take(8)
     w4 = take(4)
-    pc, pb = take(2)
+    pc, pb, unit = take(3)
     send_sem, recv_sem, gather_send, gather_recv, local_sem = take(5)
 
     gx, gy = lax.axis_index("gx"), lax.axis_index("gy")
@@ -342,82 +356,94 @@
     everything = []
 
     class Exchange:
-        def __init__(self, level, ref, wide, reach=1, faces=True, direct=False):
+        def __init__(self, *parts, reach=1, direct=False):
             self.direct = direct
-            lo, bx, by = level.halo, level.bx, level.by
-            if reach == 1:
-                up = ((lo + bx - wide, lo - wide), (lo, lo + bx))
-            else:
-                up = ((lo + 2 * bx - lo, 0), (lo, lo + 2 * bx))
+            on_x, on_y = (lambda p: (p >= 0) & (p < nx)), (lambda p: (p >= 0) & (p < ny))
+
+            def layers(level, sign, a, b):
+                lo, bx = level.halo, level.bx
+                if sign > 0:
+                    return lo + reach * bx - b, lo - b, b - a + 1
+                return lo + a - 1 - (reach - 1) * bx, lo + bx + a - 1, b - a + 1
+
+            def bundle(pairs, target, sends, receives):
+                total = sum(
+                    src.shape[0] * src.shape[1] * src.shape[2] for src, _ in pairs
+                )
+                return Bundle(pairs, target, sends, receives, total // 8, unit, sems())
+
             self.x, self.y, self.corners = [], [], []
-            own = pl.ds(8, by)
-            for sign, (src, dst) in zip((1, -1), up):
+            for sign in (1, -1):
                 there, back = gx + sign * reach, gx - sign * reach
-                ok = lambda p: (p >= 0) & (p < nx)
-                self.x.append(
-                    Copy(
-                        ref.at[pl.ds(src, wide), :, own, :],
-                        ref.at[pl.ds(dst, wide), :, own, :],
-                        (there, gy),
-                        ok(there),
-                        ok(back),
-                        sems(),
+                pairs = []
+                for level, src, dst, a, b, faces, corner in parts:
+                    at, to, count = layers(level, sign, a, b)
+                    own = pl.ds(8, level.by)
+                    pairs.append(
+                        (src.at[pl.ds(at, count), :, own, :], dst.at[pl.ds(to, count), :, own, :])
                     )
-                )
-            rows = 4 if level.nh == 2 else 8
-            sides = ((1, 8 + by - rows, 8 - rows), (-1, 8, 8 + by))
-            inside_x, inside_y = (lambda p: (p >= 0) & (p < nx)), (lambda p: (p >= 0) & (p < ny))
-            for sign, src, dst in sides:
+                self.x.append(bundle(pairs, (there, gy), on_x(there), on_x(back)))
+            for sign in (1, -1):
                 there, back = gy + sign, gy - sign
-                sends, receives = inside_y(there), inside_y(back)
-
-                def strip(start, count, row):
-                    return ref.at[pl.ds(start, count), :, pl.ds(row, rows), :]
-
-                if faces:
-                    self.y.append(
-                        Copy(
-                            strip(lo, bx, src),
-                            strip(lo, bx, dst),
-                            (gx, there),
-                            sends,
-                            receives,
-                            sems(),
+                pairs, corner_pairs = [], ([], [])
+                for level, src, dst, a, b, faces, corner in parts:
+                    deep = 4 if level.nh == 2 else 8
+                    row = 8 + level.by - deep if sign > 0 else 8
+                    to_row = 8 - deep if sign > 0 else 8 + level.by
+
+                    def strips(ref, at, to, count):
+                        return (
+                            ref.at[pl.ds(at, count), :, pl.ds(row, deep), :],
+                            dst.at[pl.ds(to, count), :, pl.ds(to_row, deep), :],
                         )
-                    )
-                for sign_x, (src_x, dst_x) in zip((1, -1), up):
-                    far, near = gx + sign_x * reach, gx - sign_x * reach
-                    have = receives & inside_x(near)
-                    self.corners.append(
-                        Copy(
-                            strip(src_x if direct else dst_x, wide, src),
-                            strip(dst_x, wide, dst),
-                            (far if direct else gx, there),
-                            sends & inside_x(far if direct else near),
-                            have,
-                            sems(),
+
+                    if faces:
+                        pairs.append(strips(src, level.halo, level.halo, level.bx))
+                    if corner:
+                        for i, sign_x in enumerate((1, -1)):
+                            at, to, count = layers(level, sign_x, *corner)
+                            corner_pairs[i].append(strips(src if direct else dst, at if direct else to, to, count))
+                if pairs:
+                    self.y.append(bundle(pairs, (gx, there), on_y(there), on_y(back)))
+                for i, sign_x in enumerate((1, -1)):
+                    if corner_pairs[i]:
+                        far, near = gx + sign_x * reach, gx - sign_x * reach
+                        self.corners.append(
+                            bundle(
+                                corner_pairs[i],
+                                (far if direct else gx, there),
+                                on_y(there) & on_x(far if direct else near),
+                                on_y(back) & on_x(near),
+                            )
                         )
-                    )
             everything.append(self)
 
         def send(self):
-            for copy in self.x + self.y + (self.corners if self.direct else []):
-                copy.start()
+            for copies in self.x + self.y + (self.corners if self.direct else []):
+                copies.start()
+
+        def rows(self):
+            for copies in self.y:
+                copies.arrive()
 
         def forward(self):
-            for copy in self.x:
-                copy.arrive()
-            for copy in [] if self.direct else self.corners:
-                copy.start()
+            for copies in self.x:
+                copies.arrive()
+            for copies in self.corners:
+                copies.arrive() if self.direct else copies.start()
 
         def finish(self):
-            for copy in self.y + self.corners:
-                copy.arrive()
+            self.rows()
+            self.last()
+
+        def last(self):
+            for copies in [] if self.direct else self.corners:
+                copies.arrive()
 
         def leave(self):
             everything.remove(self)
-            for copy in self.x + self.y + self.corners:
-                copy.leave()
+            for copies in self.x + self.y + self.corners:
+                copies.leave()
 
     class Gather:
         def __init__(self, rows, full, pad, index):
@@ -469,20 +495,29 @@
             self.first_all.wait_send()
             self.second_all.wait_send()
 
-    x_v0, x_c0, x_b0 = Exchange(l0, va0, 4), Exchange(l0, c0, 4), Exchange(l0, b0, 3)
-    x_k0 = Exchange(l0, vc0, 3)
-    x_c1, x_b1, x_k1 = Exchange(l1, c1, 5), Exchange(l1, b1, 4, direct=True), Exchange(l1, vc1, 5)
-    x_c2, x_k2 = Exchange(l2, c2, 4), Exchange(l2, vc2, 4)
-    x_b2 = Exchange(l2, b2, 4, direct=True)
-    f_c2, f_b2, f_k2 = (Exchange(l2, ref, 2, 2, False) for ref in (c2, b2, vc2))
+    x_0 = Exchange(
+        (l0, c0, c0, 1, 2, True, (1, 1)),
+        (l0, va0, va0, 1, 2, True, (1, 1)),
+        (l0, b0, b0, 1, 1, True, None),
+        direct=True,
+    )
+    x_v = Exchange((l0, ve0, ve0, 1, 2, True, (1, 1)), direct=True)
+    x_late = Exchange((l0, c0, c0, 3, 3, False, (2, 3)), (l0, b0, b0, 2, 2, False, (1, 2)))
+    x_k0 = Exchange((l0, vf0, vc0, 1, 3, True, (1, 3)))
+    x_c = Exchange((l1, c1, c1, 1, 5, True, (1, 5)), (l2, c2, c2, 1, 4, True, (1, 4)))
+    f_c = Exchange((l2, c2, c2, 5, 6, False, (5, 6)), reach=2)
+    x_b1 = Exchange((l1, b1, b1, 1, 4, True, (1, 4)), direct=True)
+    x_b2 = Exchange((l2, b2, b2, 1, 4, True, (1, 4)), direct=True)
+    x_k = Exchange((l1, vc1, vc1, 1, 5, True, (1, 5)), (l2, vc2, vc2, 1, 4, True, (1, 4)))
+    f_k = Exchange(
+        (l2, b2, b2, 5, 6, False, (5, 6)), (l2, vc2, vc2, 5, 6, False, (5, 6)), reach=2
+    )
     g_c3, g_b3 = Gather(pc, c3, l3.pad, 0), Gather(pb, b3, l3.pad, 2)
 
     for copy in loads:
         copy.wait()
     pl.semaphore_wait(barrier, nx + ny + 2)
 
-    x_c0.send()
-    x_v0.send()
 
     def double(k):
         for h in range(2):
@@ -490,7 +525,7 @@
             b0[own] = 2.0 * b0[own]
 
     loop_pieces(l0.bx, 4, double)
-    x_b0.send()
+    x_0.send()
 
     def clear(level, refs, far):
         lo, bx, by = level.halo, level.bx, level.by
@@ -514,7 +549,7 @@
         pl.when(gy == 0)(lambda: rows(0, 8))
         pl.when(gy == ny - 1)(lambda: rows(8 + by, 8))
 
-    clear(l0, (va0, c0, b0, vc0), False)
+    clear(l0, (va0, c0, b0, vc0, ve0), False)
     clear(l1, (c1, b1, vc1), False)
     clear(l2, (c2, b2, vc2), True)
     for ref in (va3, vb3, c3, va4, vb4, c4):
@@ -537,11 +572,10 @@
 
     field_pairs(l0, c0, s0)
     c1[l1.halo : l1.halo + l1.bx, 0, 8 : 8 + l1.by, :] = halve(l0, s0, 0.125)
-    x_c1.send()
     field_pairs(l1, c1, s1)
     c2[l2.halo : l2.halo + l2.bx, 0, 8 : 8 + l2.by, :] = halve(l1, s1, 0.125)
-    x_c2.send()
-    f_c2.send()
+    x_c.send()
+    f_c.send()
     for k in range(2):
         s2[pl.ds(8 * k, 8), :] = (
             c2[l2.halo + 2 * k, 0, pl.ds(8, 8), :] + c2[l2.halo + 2 * k + 1, 0, pl.ds(8, 8), :]
@@ -549,34 +583,51 @@
     g_c3.send(tile_of(s2, 0.125))
 
     bx0, by0 = gx * l0.bx, gy * l0.by
-    chain = (va0, vb0, ve0, vf0)
-    inner = tiles(12, 24)
-    setup(l0, c0, g0, d0, (1, l0.bx - 1), inner, bx0, by0)
-    for k in range(1, 4):
-        sweep(l0, chain[k - 1], chain[k], c0, g0, b0, (k, l0.bx - k), inner)
-    x_c0.forward()
-    for span in ((-3, 1), (l0.bx - 1, l0.bx + 3)):
-        setup(l0, c0, g0, d0, span, inner, bx0, by0)
-    x_v0.forward()
-    x_b0.forward()
-    for k in range(1, 4):
-        for span in ((k - 4, k), (l0.bx - k, l0.bx + 4 - k)):
-            sweep(l0, chain[k - 1], chain[k], c0, g0, b0, span, inner)
-    for exchange in (x_c0, x_v0, x_b0):
-        exchange.finish()
+    chain, bx = (va0, vb0, ve0, vf0), l0.bx
+    inner, outer, own, whole = tiles(12, 24), ((4, 8), (36, 8)), tiles(8, 32), tiles(4, 40)
+
+    def prepare(span, rows):
+        setup(l0, c0, g0, d0, span, rows, bx0, by0)
+
+    def relax(k, span, rows):
+        sweep(l0, chain[k - 1], chain[k], c0, g0, b0, span, rows)
+
+    def rest(span):
+        residual_pairs(l0, vf0, c0, b0, d0, s0, vc0, span)
+
+    edges = (((-1, 0), own), ((0, 1), whole), ((bx - 1, bx), whole), ((bx, bx + 1), own))
+    prepare((1, bx - 1), inner)
+    relax(1, (1, bx - 1), inner)
+    relax(2, (2, bx - 2), inner)
+    x_0.rows()
+    prepare((1, bx - 1), outer)
+    relax(1, (1, bx - 1), outer)
+    relax(2, (2, bx - 2), ((8, 8), (32, 8)))
+    x_0.forward()
+    for span, rows in edges:
+        prepare(span, rows)
+        relax(1, span, rows)
+    for span in ((0, 2), (bx - 2, bx)):
+        relax(2, span, own)
+    x_v.send()
+    x_late.send()
+    relax(3, (1, bx - 1), inner)
     g_c3.forward()
-    for exchange in (x_c1, x_c2, f_c2):
-        exchange.forward()
-    setup(l0, c0, g0, d0, (-3, l0.bx + 3), ((4, 8), (36, 8)), bx0, by0)
-    for k in range(1, 4):
-        span = (k - 4, l0.bx + 4 - k)
-        sweep(l0, chain[k - 1], chain[k], c0, g0, b0, span, ((3 + k, 8), (37 - k, 8)))
-    residual_pairs(l0, vf0, c0, b0, d0, s0, vc0)
+    x_c.forward()
+    f_c.forward()
+    x_v.rows()
+    relax(3, (1, bx - 1), outer)
+    rest((1, bx // 2 - 1))
+    x_v.forward()
+    for span, rows in edges:
+        relax(3, span, rows)
+    for span in ((0, 1), (bx // 2 - 1, bx // 2)):
+        rest(span)
     b1[l1.halo : l1.halo + l1.bx, 0, 8 : 8 + l1.by, :] = halve(l0, s0, 0.5)
     x_b1.send()
-    x_k0.send()
-    for exchange in (x_c1, x_c2, f_c2):
-        exchange.finish()
+    x_late.forward()
+    x_c.finish()
+    f_c.finish()
     rows1, rows2 = tiles(4, 24, 24), tiles(2, 24, 24)
     setup(l1, c1, g1, d1, (-4, l1.bx + 4), rows1, gx * l1.bx, gy * l1.by)
     setup(l2, c2, g2, d2, (-5, l2.bx + 5), rows2, gx * l2.bx, gy * l2.by)
@@ -588,8 +639,6 @@
     residual_pairs(l1, va1, c1, b1, d1, s1, vc1)
     b2[l2.halo : l2.halo + l2.bx, 0, 8 : 8 + l2.by, :] = halve(l1, s1, 0.5)
     x_b2.send()
-    f_b2.send()
-    x_k1.send()
 
     def pairs_of(ref):
         for k in range(nx):
@@ -605,6 +654,7 @@
 
     x_b2.forward()
     x_b2.finish()
+    x_k0.send()
     first_sweep(l2, va2, g2, b2, (-3, l2.bx + 3), rows2)
     sweep(l2, va2, vb2, c2, g2, b2, (-2, l2.bx + 2), rows2)
     sweep(l2, vb2, va2, c2, g2, b2, (-1, l2.bx + 1), rows2)
@@ -617,14 +667,15 @@
             total = part if total is None else total + part
         s2[pl.ds(8 * k, 8), :] = total[0, 0]
     g_b3.send(tile_of(s2, 0.5))
-    x_k2.send()
-    f_k2.send()
+    x_k.send()
+    f_k.send()
+    g_b3.forward()
+    x_late.finish()
+    for span in ((-2, 0), (bx, bx + 2)):
+        prepare(span, whole)
     x_k0.forward()
-    x_k1.forward()
-    f_b2.forward()
-    g_b3.forward()
-    x_k2.forward()
-    f_k2.forward()
+    x_k.forward()
+    f_k.forward()
     g_b3.finish()
     for k in range(l3.count):
         va3[l3.pad + k] = g3[k] * b3[l3.pad + k]
@@ -674,9 +725,8 @@
     packed_sweep(l3, va3, vb3, w3, wx3, g3, b3, l3.pad)
     packed_sweep(l3, vb3, va3, w3, wx3, g3, b3, l3.pad)
 
-    f_b2.finish()
-    x_k2.finish()
-    f_k2.finish()
+    f_k.finish()
+    x_k.finish()
     group = lax.shift_right_logical(gy, 1) - 1
     e3 = va3[pl.ds(l3.pad - 3 + 2 * gx, 8)].reshape(64, LANES)
     for q in range(3):
@@ -688,7 +738,6 @@
     sweep(l2, vb2, va2, c2, g2, b2, (-4, l2.bx + 4), rows2)
     sweep(l2, va2, vb2, c2, g2, b2, (-3, l2.bx + 3), rows2)
 
-    x_k1.finish()
     prolong(l1, vb2, 3, 4, 10, 16, pe1, None, None, 0)
     add_prolonged(l1, pe1, vc1, va1, 0, 0, 10, 16)
     sweep(l1, va1, vb1, c1, g1, b1, (-4, l1.bx + 4), rows1)
@@ -697,7 +746,8 @@
 
     x_k0.finish()
     prolong(l0, vb1, 4, 4, 12, 24, pe0, None, None, 0)
-    x_v0.leave()
+    x_0.leave()
+    x_v.leave()
     add_prolonged(l0, pe0, vc0, va0, 0, 0, 12, 24)
     def put(x0, r, n, new):
         for h in range(2):
@@ -731,8 +781,8 @@
     scratch += [e(l3)] * 4 + [l3.own(1), o(l3), o(l3), vmem(nx, 16, LANES), vmem(nx, 8, LANES)]
     scratch += [o(l3)] * 4
     scratch += [e(l4)] * 3 + [l4.own(1)] + [o(l4)] * 8
-    scratch += [vmem(ny, 8, LANES)] * 2
-    copies = 10 * 8 + 3 * 6
+    scratch += [vmem(ny, 8, LANES)] * 2 + [vmem(64, 8, LANES)]
+    copies = 7 * 8 + 3 * 6
     scratch += [
         pltpu.SemaphoreType.DMA((copies,)),
         pltpu.SemaphoreType.DMA((copies,)),

time: 54.1 us -> 51.3 us (0.948)
  Pallas kernels: 53.2 us -> 50.4 us
    pallas_call x1, Pallas kernels: 53.2 us -> 50.4 us  [step(): pl.pallas_call(functools.partial(kernel, nx, ny, (l0, l1, l2, l3, l4)), o...]
where the time goes in v4:
time: 51.3 us; the launch traced here: 51.2 us
  Pallas kernels  50.4 us (98%)
  local copies, waits for them, and re-layouts  0.8 us (2%)
    pallas_call x1, Pallas kernels, step(): pl.pallas_call(functools.partial(kernel, nx, ny, (l0, l1, l2, l3, l4)), o...  50.4 us

profile of v4, /device:TPU:0, one launch (start us, length us, event | category | flops | bytes accessed | tf_op | source)
XLA Modules:
  0.0 51.2 jit_solution(4060354943467123585)
XLA Ops:
  0.0 50.4 %shard_map.37 = f32[16,32,256]{2,1,0:T(8,128)S(1)} custom-call(f32[16,32,256]{2,1,0:T(8,128)} %guess.1, f32[16,32,256]{2,1,0:T(8,128)} %rhs.1, f32[16,32,256]{2,1,0:T(8,128)} %coef.1), custom_call_target="tpu_custom_call" | custom-call | tf_op jit(solution)/shard_map/pallas_call | solution.py:795
  50.4 0.8 %copy.5 = f32[16,32,256]{2,1,0:T(8,128)} copy(f32[16,32,256]{2,1,0:T(8,128)S(1)} %shard_map.37) | data formatting | bytes 1048576

commit v5 on v4

--- a/solution.py
+++ b/solution.py
@@ -1,4 +1,5 @@
 import functools
+import math
 
 import jax
 import jax.numpy as jnp
@@ -154,7 +155,14 @@
 
 
 def dot(a, m):
-    return jnp.dot(a, m, precision=lax.Precision.HIGHEST, preferred_element_type=F32)
+    half = jnp.bfloat16
+    high = a.astype(half)
+    rest = a - high.astype(F32)
+    middle = rest.astype(half)
+    low = (rest - middle.astype(F32)).astype(half)
+    m = m.astype(half)
+    parts = [jnp.dot(p, m, preferred_element_type=F32) for p in (low, middle, high)]
+    return (parts[0] + parts[1]) + parts[2]
 
 
 def halve(level, s, weight):
@@ -262,7 +270,7 @@
         new = (1.0 - RELAX) * v + g[pl.ds(k, 1)] * (t + b[pl.ds(b_pad + k, 1)])
         dst[pl.ds(p.pad + k, 1)] = new
 
-    loop_pieces(p.count, 16, body)
+    loop_pieces(p.count, p.count, body)
 
 
 def packed_halve(s, weight):
@@ -322,8 +330,8 @@
     gx, gy = lax.axis_index("gx"), lax.axis_index("gy")
     counter = iter(range(1000))
 
-    def sems():
-        return send_sem, recv_sem, next(counter)
+    def sems(again=None):
+        return send_sem, recv_sem, next(counter if again is None else again)
 
     loads = []
     for i, (src, dst) in enumerate(((coef, c0), (guess, va0), (rhs, b0))):
@@ -356,8 +364,10 @@
     everything = []
 
     class Exchange:
-        def __init__(self, *parts, reach=1, direct=False):
+        def __init__(self, *parts, reach=1, direct=False, after=None):
             self.direct = direct
+            again = None if after is None else iter(after.indices)
+            self.indices = []
             on_x, on_y = (lambda p: (p >= 0) & (p < nx)), (lambda p: (p >= 0) & (p < ny))
 
             def layers(level, sign, a, b):
@@ -367,10 +377,10 @@
                 return lo + a - 1 - (reach - 1) * bx, lo + bx + a - 1, b - a + 1
 
             def bundle(pairs, target, sends, receives):
-                total = sum(
-                    src.shape[0] * src.shape[1] * src.shape[2] for src, _ in pairs
-                )
-                return Bundle(pairs, target, sends, receives, total // 8, unit, sems())
+                total = sum(math.prod(dst.shape) for _, dst in pairs) // (8 * LANES)
+                chosen = sems(again)
+                self.indices.append(chosen[2])
+                return Bundle(pairs, target, sends, receives, total, unit, chosen)
 
             self.x, self.y, self.corners = [], [], []
             for sign in (1, -1):
@@ -506,11 +516,13 @@
     x_k0 = Exchange((l0, vf0, vc0, 1, 3, True, (1, 3)))
     x_c = Exchange((l1, c1, c1, 1, 5, True, (1, 5)), (l2, c2, c2, 1, 4, True, (1, 4)))
     f_c = Exchange((l2, c2, c2, 5, 6, False, (5, 6)), reach=2)
-    x_b1 = Exchange((l1, b1, b1, 1, 4, True, (1, 4)), direct=True)
-    x_b2 = Exchange((l2, b2, b2, 1, 4, True, (1, 4)), direct=True)
-    x_k = Exchange((l1, vc1, vc1, 1, 5, True, (1, 5)), (l2, vc2, vc2, 1, 4, True, (1, 4)))
+    x_b1 = Exchange((l1, b1, b1, 1, 4, True, (1, 4)), direct=True, after=x_0)
+    x_b2 = Exchange((l2, b2, b2, 1, 4, True, (1, 4)), direct=True, after=x_v)
+    x_k = Exchange((l1, vc1, vc1, 1, 5, True, (1, 5)), (l2, vc2, vc2, 1, 4, True, (1, 4)),
+        after=x_c,
+    )
     f_k = Exchange(
-        (l2, b2, b2, 5, 6, False, (5, 6)), (l2, vc2, vc2, 5, 6, False, (5, 6)), reach=2
+        (l2, b2, b2, 5, 6, False, (5, 6)), (l2, vc2, vc2, 5, 6, False, (5, 6)), reach=2, after=f_c
     )
     g_c3, g_b3 = Gather(pc, c3, l3.pad, 0), Gather(pb, b3, l3.pad, 2)
 
@@ -624,6 +636,7 @@
     for span in ((0, 1), (bx // 2 - 1, bx // 2)):
         rest(span)
     b1[l1.halo : l1.halo + l1.bx, 0, 8 : 8 + l1.by, :] = halve(l0, s0, 0.5)
+    x_0.leave()
     x_b1.send()
     x_late.forward()
     x_c.finish()
@@ -638,6 +651,7 @@
     sweep(l1, vb1, va1, c1, g1, b1, (-1, l1.bx + 1), rows1)
     residual_pairs(l1, va1, c1, b1, d1, s1, vc1)
     b2[l2.halo : l2.halo + l2.bx, 0, 8 : 8 + l2.by, :] = halve(l1, s1, 0.5)
+    x_v.leave()
     x_b2.send()
 
     def pairs_of(ref):
@@ -667,13 +681,14 @@
             total = part if total is None else total + part
         s2[pl.ds(8 * k, 8), :] = total[0, 0]
     g_b3.send(tile_of(s2, 0.5))
+    x_c.leave()
+    f_c.leave()
     x_k.send()
     f_k.send()
     g_b3.forward()
     x_late.finish()
     for span in ((-2, 0), (bx, bx + 2)):
         prepare(span, whole)
-    x_k0.forward()
     x_k.forward()
     f_k.forward()
     g_b3.finish()
@@ -694,6 +709,7 @@
     loop_pieces(nx, 2, residual3)
     res4[...] = packed_halve(s3, 0.5)
 
+    x_k0.forward()
     sigma = THETA / DELTA
     rho = 1.0 / sigma
     for k in range(nx):
@@ -746,8 +762,6 @@
 
     x_k0.finish()
     prolong(l0, vb1, 4, 4, 12, 24, pe0, None, None, 0)
-    x_0.leave()
-    x_v.leave()
     add_prolonged(l0, pe0, vc0, va0, 0, 0, 12, 24)
     def put(x0, r, n, new):
         for h in range(2):
@@ -782,7 +796,7 @@
     scratch += [o(l3)] * 4
     scratch += [e(l4)] * 3 + [l4.own(1)] + [o(l4)] * 8
     scratch += [vmem(ny, 8, LANES)] * 2 + [vmem(64, 8, LANES)]
-    copies = 7 * 8 + 3 * 6
+    copies = 4 * 8 + 2 * 6
     scratch += [
         pltpu.SemaphoreType.DMA((copies,)),
         pltpu.SemaphoreType.DMA((copies,)),

time: 51.3 us -> 49.9 us (0.973)
  Pallas kernels: 50.4 us -> 48.9 us
    pallas_call x1, Pallas kernels: 50.4 us -> 48.9 us  [step(): pl.pallas_call(functools.partial(kernel, nx, ny, (l0, l1, l2, l3, l4)), o...]
where the time goes in v5:
time: 49.9 us; the launch traced here: 49.7 us
  Pallas kernels  48.9 us (98%)
  local copies, waits for them, and re-layouts  0.8 us (2%)
    pallas_call x1, Pallas kernels, step(): pl.pallas_call(functools.partial(kernel, nx, ny, (l0, l1, l2, l3, l4)), o...  48.9 us

profile of v5, /device:TPU:0, one launch (start us, length us, event | category | flops | bytes accessed | tf_op | source)
XLA Modules:
  0.0 49.7 jit_solution(11441530953520694025)
XLA Ops:
  0.0 48.9 %shard_map.37 = f32[16,32,256]{2,1,0:T(8,128)S(1)} custom-call(f32[16,32,256]{2,1,0:T(8,128)} %guess.1, f32[16,32,256]{2,1,0:T(8,128)} %rhs.1, f32[16,32,256]{2,1,0:T(8,128)} %coef.1), custom_call_target="tpu_custom_call" | custom-call | tf_op jit(solution)/shard_map/pallas_call | solution.py:809
  48.9 0.8 %copy.5 = f32[16,32,256]{2,1,0:T(8,128)} copy(f32[16,32,256]{2,1,0:T(8,128)S(1)} %shard_map.37) | data formatting | bytes 1048576

commit v6 on v5

--- a/solution.py
+++ b/solution.py
@@ -15,7 +15,7 @@
 THETA = 1.04
 DELTA = 0.96
 LANES = 128
-REGISTERS = 120
+REGISTERS = 260
 
 
 def iota(shape, dim):

time: 49.9 us -> 49.5 us (level)
  no operation moved by 1% of the time
where the time goes in v6:
time: 49.5 us; the launch traced here: 49.3 us
  Pallas kernels  48.5 us (98%)
  local copies, waits for them, and re-layouts  0.8 us (2%)
    pallas_call x1, Pallas kernels, step(): pl.pallas_call(functools.partial(kernel, nx, ny, (l0, l1, l2, l3, l4)), o...  48.5 us

profile of v6, /device:TPU:0, one launch (start us, length us, event | category | flops | bytes accessed | tf_op | source)
XLA Modules:
  0.0 49.3 jit_solution(9903849852954505736)
XLA Ops:
  0.0 48.5 %shard_map.37 = f32[16,32,256]{2,1,0:T(8,128)S(1)} custom-call(f32[16,32,256]{2,1,0:T(8,128)} %guess.1, f32[16,32,256]{2,1,0:T(8,128)} %rhs.1, f32[16,32,256]{2,1,0:T(8,128)} %coef.1), custom_call_target="tpu_custom_call" | custom-call | tf_op jit(solution)/shard_map/pallas_call | solution.py:809
  48.5 0.8 %copy.5 = f32[16,32,256]{2,1,0:T(8,128)} copy(f32[16,32,256]{2,1,0:T(8,128)S(1)} %shard_map.37) | data formatting | bytes 1048576
